TPU v7x, 32 devices: a whole 2x2x4 slice. The times are simulated.
32 devices in a mesh: member: 8 (over z, x), space: 4 (over y, core).
Axes of the slice: x: 2, y: 2, z: 4, core: 2. Of those that a mesh axis runs over, the one named last changes fastest.
Arguments:
- alpha: float32 [16, 16, 32, 1280], P('member', None, 'space'), may hold values from -6 to 6
- perturb: bfloat16 [4, 16, 16, 32, 1280], P(None, 'member', None, 'space'), may hold values from -1.5 to 1.5
- kappa: float32 [32, 1280], P('space'), may hold values from 0.1 to 0.24
- land: int32 [32, 1280], P('space'), may hold values 0 or 1
- obs_weight: float32 [4, 16, 32, 1280], P(None, 'member', 'space'), may hold values from 0.2 to 5
- innovation: float32 [4, 16, 32, 1280], P(None, 'member', 'space'), may hold values from -6 to 6
Outputs:
- gradient: float32 [16, 16, 32, 1280], P('member', None, 'space')
- weighted_misfit: float32 [4, 16, 32, 1280], P(None, 'member', 'space')
All inputs are finite; a program needn't handle non-finite values. No bound on the sum of `land` on one device may be relied on, other than what follows from the above.
Results may differ from a plain program's by a relative error of at most 0.0003.
Values sent between devices are 32-bit elements; how exact they have to be, the bound alone decides.
No kernel may reach another device: no remote copies, remote signals or barrier semaphores. Data moves between devices by JAX's collectives and lax.ppermute only.
A program may use at most 64 MiB of HBM per device.

v0:
```python
import functools

import jax
import jax.numpy as jnp
from jax import lax
from jax.experimental import pallas as pl
from jax.experimental.pallas import tpu as pltpu
from jax.sharding import PartitionSpec as P


STEPS = 4
F32 = jnp.float32


def fill_faces(faces, kappa, beyond):
    width = kappa.shape[-1]
    row = lax.broadcasted_iota(jnp.int32, kappa.shape, 0)
    last = row == kappa.shape[0] - 1
    here, there = pltpu.roll(kappa, 7, 0), pltpu.roll(beyond, 7, 0)
    faces[0] = 0.5 * (kappa + pltpu.roll(kappa, width - 1, 1))
    faces[1] = 0.5 * (beyond + pltpu.roll(beyond, width - 1, 1))
    faces[2] = 0.5 * (kappa + jnp.where(last, there, here))
    faces[3] = 0.5 * (beyond + jnp.where(last, here, there))
    place, count = lax.axis_index("space"), lax.axis_size("space")
    has_above = (place < count - 1).astype(F32)
    has_below = (place > 0).astype(F32)
    faces[4] = jnp.where(row < 4, has_above, has_below)


def diffuse(faces, u, h):
    width = u.shape[-1]
    row = lax.broadcasted_iota(jnp.int32, u.shape, 0)
    last, first = row == u.shape[0] - 1, row == 0

    def along(v, face):
        flux = face * (pltpu.roll(v, width - 1, 1) - v)
        return flux - pltpu.roll(flux, 1, 1)

    for sweep in range(STEPS):
        ru, rh = pltpu.roll(u, 7, 0), pltpu.roll(h, 7, 0)
        fu = faces[2] * (jnp.where(last, rh, ru) - u)
        fh = faces[3] * (jnp.where(last, ru, rh) - h)
        su, sh = pltpu.roll(fu, 1, 0), pltpu.roll(fh, 1, 0)
        v = u + along(u, faces[0]) + (fu - jnp.where(first, sh, su))
        if sweep < STEPS - 1:
            h = faces[4] * (h + along(h, faces[1]) + (fh - jnp.where(first, su, sh)))
        u = v
    return u


def place_of(index, bits):
    owner = 0
    for k, bit in enumerate(reversed(bits)):
        owner = owner + ((index >> k) & 1) * bit
    return owner


def index_of(owner, bits):
    index = 0
    for bit in bits:
        index = index * 2 + jnp.where((owner & bit) != 0, 1, 0)
    return index


def forward_kernel(chunk, width, groups, alpha, beyond, k_beyond, kappa, land, perturb, *refs):
    faces, outs = refs[-1], refs[:-1]
    members = perturb.shape[1]
    count = 2 * outs[0].shape[0]
    me = lax.axis_index("member")
    fill_faces(faces, kappa[...], k_beyond[...])
    lead = groups[0][1]
    for half in (1, 0):
        def level(i, carry, half=half):
            owner = place_of(i, lead[1:]) + half * lead[0]
            piece = owner ^ me
            row = piece * width + chunk
            local = []
            for m in range(members):
                local.append(diffuse(faces, alpha[m, row], beyond[m * count + piece]) * land[...].astype(F32))

            def added(t):
                total = perturb[t, 0, row].astype(F32) * local[0]
                for m in range(1, members):
                    total = total + perturb[t, m, row].astype(F32) * local[m]
                return total

            for g, (slots, order) in enumerate(groups):
                send, keep = outs[2 * g : 2 * g + 2]
                if order == lead:
                    for k, t in enumerate(slots):
                        (send if half else keep)[i, k] = added(t)
                else:
                    at = index_of(owner, order[1:])
                    sends = (owner & order[0]) != 0
                    values = [added(t) for t in slots]

                    @pl.when(sends)
                    def _(values=values, send=send, at=at):
                        for k, value in enumerate(values):
                            send[at, k] = value

                    @pl.when(jnp.logical_not(sends))
                    def _(values=values, keep=keep, at=at):
                        for k, value in enumerate(values):
                            keep[at, k] = value
            return carry

        lax.fori_loop(0, count // 2, level, 0)


def back_kernel(chunk, width, groups, perturb, land, *refs):
    back, to_partner, to_next = refs[-3:]
    given = refs[:-3]
    members = perturb.shape[1]
    count = 2 * given[0].shape[0]
    me = lax.axis_index("member")
    even = lax.rem(lax.axis_index("space"), 2) == 0
    lead = groups[0][1]
    for half in (0, 1):
        def level(i, carry, half=half):
            owner = place_of(i, lead[1:]) + half * lead[0]
            piece = owner ^ me
            row = piece * width + chunk
            sea = land[...].astype(F32)
            totals = [None] * members
            for g, (slots, order) in enumerate(groups):
                low, high = given[2 * g : 2 * g + 2]
                for k, t in enumerate(slots):
                    if order == lead:
                        value = (high if half else low)[i, k]
                    else:
                        at = index_of(owner, order[1:])
                        value = jnp.where((owner & order[0]) != 0, high[at, k], low[at, k])
                    for m in range(members):
                        term = perturb[t, m, row].astype(F32) * value
                        totals[m] = term if totals[m] is None else totals[m] + term
            for m in range(members):
                total = totals[m] * sea
                back[m, piece] = total
                to_partner[m * count + piece] = jnp.where(even, total[4:], total[:4])
                to_next[m * count + piece] = jnp.where(even, total[:4], total[4:])
            return carry

        lax.fori_loop(0, count // 2, level, 0)


def adjoint_kernel(chunk, width, alpha, back, beyond, k_beyond, kappa, *refs):
    gradient, faces, stage, done = refs[-4:]
    members, count = back.shape[:2]
    fill_faces(faces, kappa[...], k_beyond[...])

    def copy(m, piece):
        return pltpu.make_async_copy(
            stage.at[m, piece], gradient.at[m, piece * width + chunk], done.at[m, piece]
        )

    def level(piece, carry):
        for m in range(members):
            value = diffuse(faces, back[m, piece], beyond[m * count + piece])
            stage[m, piece] = value + alpha[m, piece * width + chunk]
            copy(m, piece).start()
        return carry

    def finish(piece, carry):
        for m in range(members):
            copy(m, piece).wait()
        return carry

    lax.fori_loop(0, count, level, 0)
    lax.fori_loop(0, count, finish, 0)


VMEM = pl.BlockSpec(memory_space=pltpu.VMEM)
GRANT = pltpu.CompilerParams(vmem_limit_bytes=24 << 20)


def call(kernel, args, outs, scratch=()):
    return pl.pallas_call(
        kernel,
        out_shape=[jax.ShapeDtypeStruct(shape, F32) for shape in outs],
        in_specs=[VMEM] * len(args),
        out_specs=[VMEM] * len(outs),
        scratch_shapes=[pltpu.VMEM(shape, F32) for shape in scratch],
        compiler_params=GRANT,
    )(*args)


def exchange(x, bit):
    count = lax.axis_size("member")
    return lax.ppermute(x, "member", [(i, i ^ bit) for i in range(count)])


def halves(to_partner, to_next):
    ends = lax.axis_size("space")
    pairs = [(i, i ^ 1) for i in range(ends)]
    nexts = [(i, i + 1 if i % 2 else i - 1) for i in range(1, ends - 1)]
    near = lax.ppermute(to_partner, "space", pairs)
    far = lax.ppermute(to_next, "space", nexts)
    even = lax.rem(lax.axis_index("space"), 2) == 0
    return jnp.concatenate([jnp.where(even, near, far), jnp.where(even, far, near)], axis=1)


def scatter(send, keep, bits):
    got = exchange(send, bits[0])
    for bit in bits[1:-1]:
        half = keep.shape[0] // 2
        send = keep[half:] + got[half:]
        keep = keep[:half] + got[:half]
        got = exchange(send, bit)
    return keep, got


def gather(held, bits):
    for k in range(len(bits) - 2, 0, -1):
        got = exchange(held, bits[k])
        held = jnp.concatenate([held, got], axis=0)
    return held, exchange(held, bits[0])


def inner(alpha, perturb, kappa, land, obs_weight, innovation):
    members, _, rows, lon = alpha.shape
    slots = perturb.shape[0]
    count = lax.axis_size("member")
    width = obs_weight.shape[1]
    bits = [1 << k for k in range(count.bit_length() - 1)]
    early, late = tuple(range(slots // 2)), tuple(range(slots // 2, slots))
    plans = [((early, bits), (late, bits)) for _ in range(width)]

    even = lax.rem(lax.axis_index("space"), 2) == 0
    split = alpha.reshape(members, count, width, rows, lon)
    beyond = []
    for c in range(width):
        mine = split[:, :, c].reshape(members * count, rows, lon)
        if c == 0:
            mine = jnp.concatenate([mine, kappa[None]], axis=0)
        low, high = mine[:, :4], mine[:, 4:]
        beyond.append(halves(jnp.where(even, high, low), jnp.where(even, low, high)))
    k_beyond = beyond[0][-1]

    far_weight = exchange(obs_weight, bits[-1])
    apart = {}
    for c in range(width):
        for g, (group, order) in enumerate(plans[c]):
            span = slice(group[0], group[-1] + 1)
            apart[c, g] = (innovation[span, c], jnp.stack([obs_weight[span, c], far_weight[span, c]]))
    apart = lax.optimization_barrier(apart)

    misfits = [[] for _ in range(width)]
    parts = [[] for _ in range(width)]
    for c in range(width):
        half = (count // 2,)
        shapes = [half + (len(group), rows, lon) for group, order in plans[c] for _ in range(2)]
        sums = call(
            functools.partial(forward_kernel, c, width, plans[c]),
            (alpha, beyond[c], k_beyond, kappa, land, perturb),
            shapes,
            [(5, rows, lon)],
        )
        for g, (group, order) in enumerate(plans[c]):
            offset, weights = apart[c, g]
            keep, got = scatter(sums[2 * g], sums[2 * g + 1], order)
            both = keep + got
            both = jnp.stack([both[0] - offset, both[1]])
            got = exchange(both, bits[-1])
            misfit = weights * (both + got[::-1])
            misfits[c].append(misfit[0])
            parts[c].extend(gather(misfit, order))

    gradient = None
    for c in range(width):
        back, to_partner, to_next = call(
            functools.partial(back_kernel, c, width, plans[c]),
            (perturb, land, *parts[c]),
            [(members, count, rows, lon)] + [(members * count, 4, lon)] * 2,
        )
        args = [alpha, back, halves(to_partner, to_next), k_beyond, kappa]
        specs = [VMEM] * len(args)
        if gradient is not None:
            args.append(gradient)
            specs.append(pl.BlockSpec(memory_space=pl.ANY))
        gradient = pl.pallas_call(
            functools.partial(adjoint_kernel, c, width),
            out_shape=jax.ShapeDtypeStruct(alpha.shape, F32),
            in_specs=specs,
            out_specs=pl.BlockSpec(memory_space=pl.ANY),
            scratch_shapes=[
                pltpu.VMEM((5, rows, lon), F32),
                pltpu.VMEM((members, count, rows, lon), F32),
                pltpu.SemaphoreType.DMA((members, count)),
            ],
            input_output_aliases={5: 0} if c else {},
            compiler_params=GRANT,
        )(*args)
    misfit = jnp.stack([jnp.concatenate(m, axis=0) for m in misfits], axis=1)
    return gradient, misfit


def solution(mesh):
    placed = (
        P("member", None, "space", None),
        P(None, "member", None, "space", None),
        P("space", None),
        P("space", None),
        P(None, "member", "space", None),
        P(None, "member", "space", None),
    )
    return jax.shard_map(
        inner,
        mesh=mesh,
        in_specs=placed,
        out_specs=(P("member", None, "space", None), P(None, "member", "space", None)),
        check_vma=False,
    )
```

profile of v0, /device:TPU:1, one launch (start us, length us, event | category | flops | bytes accessed | tf_op | source)
XLA Modules:
  0.0 139.9 jit_solution(5035545712817193931)
XLA Ops:
  1.6 3.2 %collective-permute-start = (f32[4,2,8,1280]{3,2,0,1:T(8,128)S(1)}, f32[4,2,8,1280]{3,2,0,1:T(8,128)S(1)}, u32[]{:S(2)}, u32[]{:S(2)}) collective-permute-start(f32[4,2,8,1280]{3,2,0,1:T(8,128)S(1)} %copy.10), channel_id=1, source_target_pairs={{0,16},{4,20},{8,24},{12,28},{16,0},{20,4},{24,8},{28,12},{1,17},{... | collective-permute-start | bytes 983048 | tf_op jit(solution)/shard_map/ppermute | solution.py:190
  7.4 3.0 %collective-permute-start.2 = (f32[16,4,1280]{2,1,0:T(4,128)S(1)}, f32[16,4,1280]{2,1,0:T(4,128)S(1)}, u32[]{:S(2)}, u32[]{:S(2)}) collective-permute-start(f32[16,4,1280]{2,1,0:T(4,128)S(1)} %get-tuple-element.61), channel_id=1, source_target_pairs={{1,2},{2,1},{5,6},{6,5},{9,10},{10,9},{13,14},{14,13},{17,18},{18,... | collective-permute-start | bytes 983048 | tf_op jit(solution)/shard_map/ppermute | solution.py:198
  10.6 2.5 %collective-permute-start.4 = (f32[17,4,1280]{2,1,0:T(4,128)S(1)}, f32[17,4,1280]{2,1,0:T(4,128)S(1)}, u32[]{:S(2)}, u32[]{:S(2)}) collective-permute-start(f32[17,4,1280]{2,1,0:T(4,128)S(1)} %get-tuple-element.53), channel_id=1, source_target_pairs={{1,2},{2,1},{5,6},{6,5},{9,10},{10,9},{13,14},{14,13},{17,18},{18,... | collective-permute-start | bytes 1044488 | tf_op jit(solution)/shard_map/ppermute | solution.py:198
  13.3 2.8 %collective-permute-done.2 = f32[16,4,1280]{2,1,0:T(4,128)S(1)} collective-permute-done((f32[16,4,1280]{2,1,0:T(4,128)S(1)}, f32[16,4,1280]{2,1,0:T(4,128)S(1)}, u32[]{:S(2)}, u32[]{:S(2)}) %collective-permute-start.2) | collective-permute-done | bytes 327712 | tf_op jit(solution)/shard_map/ppermute | solution.py:198
  16.1 3.1 %collective-permute-done = f32[4,2,8,1280]{3,2,0,1:T(8,128)S(1)} collective-permute-done((f32[4,2,8,1280]{3,2,0,1:T(8,128)S(1)}, f32[4,2,8,1280]{3,2,0,1:T(8,128)S(1)}, u32[]{:S(2)}, u32[]{:S(2)}) %collective-permute-start) | collective-permute-done | bytes 327712 | tf_op jit(solution)/shard_map/ppermute | solution.py:190
  21.6 5.3 %shard_map.79 = (f32[4,2,8,1280]{3,2,1,0:T(8,128)S(1)}, f32[4,2,8,1280]{3,2,1,0:T(8,128)S(1)}, f32[4,2,8,1280]{3,2,1,0:T(8,128)S(1)}, f32[4,2,8,1280]{3,2,1,0:T(8,128)S(1)}) custom-call(f32[2,16,8,1280]{3,2,1,0:T(8,128)S(1)} %copy-done.1, f32[17,8,1280]{2,1,0:T(8,128)S(1)} %pad_maximum_fusion.beyond, f32[8,1280]{1,0:T(8,128)S(1)} %fusion.14.k_beyond, ...), custom_call_target="tpu_custom_call" | custom-call | tf_op jit(solution)/shard_map/pallas_call | solution.py:178
  28.7 5.3 %shard_map.77 = (f32[4,2,8,1280]{3,2,1,0:T(8,128)S(1)}, f32[4,2,8,1280]{3,2,1,0:T(8,128)S(1)}, f32[4,2,8,1280]{3,2,1,0:T(8,128)S(1)}, f32[4,2,8,1280]{3,2,1,0:T(8,128)S(1)}) custom-call(f32[2,16,8,1280]{3,2,1,0:T(8,128)S(1)} %copy-done.1, f32[16,8,1280]{2,1,0:T(8,128)S(1)} %pad_maximum_fusion.1.beyond, f32[8,1280]{1,0:T(8,128)S(1)} %fusion.14.k_beyond, ...), custom_call_target="tpu_custom_call" | custom-call | tf_op jit(solution)/shard_map/pallas_call | solution.py:178
  37.0 5.2 %collective-permute-done.22 = f32[4,2,8,1280]{3,2,1,0:T(8,128)S(1)} collective-permute-done((f32[4,2,8,1280]{3,2,1,0:T(8,128)S(1)}, f32[4,2,8,1280]{3,2,1,0:T(8,128)S(1)}, u32[]{:S(2)}, u32[]{:S(2)}) %collective-permute-start.22) | collective-permute-done | bytes 327712 | tf_op jit(solution)/shard_map/ppermute | solution.py:190
  42.3 1.8 %collective-permute-start.23 = (f32[2,2,8,1280]{3,2,1,0:T(8,128)S(1)}, f32[2,2,8,1280]{3,2,1,0:T(8,128)S(1)}, u32[]{:S(2)}, u32[]{:S(2)}) collective-permute-start(f32[2,2,8,1280]{3,2,1,0:T(8,128)S(1)} %slice_add_fusion), channel_id=1, source_target_pairs={{0,8},{4,12},{8,0},{12,4},{16,24},{20,28},{24,16},{28,20},{1,9},{5... | collective-permute-start | bytes 491528 | tf_op jit(solution)/shard_map/ppermute | solution.py:190
  44.1 5.2 %collective-permute-done.5 = f32[4,2,8,1280]{3,2,1,0:T(8,128)S(1)} collective-permute-done((f32[4,2,8,1280]{3,2,1,0:T(8,128)S(1)}, f32[4,2,8,1280]{3,2,1,0:T(8,128)S(1)}, u32[]{:S(2)}, u32[]{:S(2)}) %collective-permute-start.5) | collective-permute-done | bytes 327712 | tf_op jit(solution)/shard_map/ppermute | solution.py:190
  49.3 1.8 %collective-permute-start.6 = (f32[2,2,8,1280]{3,2,1,0:T(8,128)S(1)}, f32[2,2,8,1280]{3,2,1,0:T(8,128)S(1)}, u32[]{:S(2)}, u32[]{:S(2)}) collective-permute-start(f32[2,2,8,1280]{3,2,1,0:T(8,128)S(1)} %slice_add_fusion.6), channel_id=1, source_target_pairs={{0,8},{4,12},{8,0},{12,4},{16,24},{20,28},{24,16},{28,20},{1,9},{5... | collective-permute-start | bytes 491528 | tf_op jit(solution)/shard_map/ppermute | solution.py:190
  51.1 5.2 %collective-permute-done.10 = f32[4,2,8,1280]{3,2,1,0:T(8,128)S(1)} collective-permute-done((f32[4,2,8,1280]{3,2,1,0:T(8,128)S(1)}, f32[4,2,8,1280]{3,2,1,0:T(8,128)S(1)}, u32[]{:S(2)}, u32[]{:S(2)}) %collective-permute-start.10) | collective-permute-done | bytes 327712 | tf_op jit(solution)/shard_map/ppermute | solution.py:190
  56.3 1.8 %collective-permute-start.11 = (f32[2,2,8,1280]{3,2,1,0:T(8,128)S(1)}, f32[2,2,8,1280]{3,2,1,0:T(8,128)S(1)}, u32[]{:S(2)}, u32[]{:S(2)}) collective-permute-start(f32[2,2,8,1280]{3,2,1,0:T(8,128)S(1)} %slice_add_fusion.4), channel_id=1, source_target_pairs={{0,8},{4,12},{8,0},{12,4},{16,24},{20,28},{24,16},{28,20},{1,9},{5... | collective-permute-start | bytes 491528 | tf_op jit(solution)/shard_map/ppermute | solution.py:190
  58.2 3.0 %collective-permute-start.19 = (f32[2,2,8,1280]{3,2,1,0:T(8,128)S(1)}, f32[2,2,8,1280]{3,2,1,0:T(8,128)S(1)}, u32[]{:S(2)}, u32[]{:S(2)}) collective-permute-start(f32[2,2,8,1280]{3,2,1,0:T(8,128)S(1)} %pad_maximum_fusion.16), channel_id=1, source_target_pairs={{0,16},{4,20},{8,24},{12,28},{16,0},{20,4},{24,8},{28,12},{1,17},{... | collective-permute-start | bytes 491528 | tf_op jit(solution)/shard_map/ppermute | solution.py:190
  61.5 2.4 %collective-permute-start.7 = (f32[2,2,8,1280]{3,2,1,0:T(8,128)S(1)}, f32[2,2,8,1280]{3,2,1,0:T(8,128)S(1)}, u32[]{:S(2)}, u32[]{:S(2)}) collective-permute-start(f32[2,2,8,1280]{3,2,1,0:T(8,128)S(1)} %pad_maximum_fusion.14), channel_id=1, source_target_pairs={{0,16},{4,20},{8,24},{12,28},{16,0},{20,4},{24,8},{28,12},{1,17},{... | collective-permute-start | bytes 491528 | tf_op jit(solution)/shard_map/ppermute | solution.py:190
  64.0 1.6 %collective-permute-start.12 = (f32[2,2,8,1280]{3,2,1,0:T(8,128)S(1)}, f32[2,2,8,1280]{3,2,1,0:T(8,128)S(1)}, u32[]{:S(2)}, u32[]{:S(2)}) collective-permute-start(f32[2,2,8,1280]{3,2,1,0:T(8,128)S(1)} %pad_maximum_fusion.15), channel_id=1, source_target_pairs={{0,16},{4,20},{8,24},{12,28},{16,0},{20,4},{24,8},{28,12},{1,17},{... | collective-permute-start | bytes 491528 | tf_op jit(solution)/shard_map/ppermute | solution.py:190
  65.7 12.2 %collective-permute-start.20 = (f32[2,2,8,1280]{3,2,1,0:T(8,128)S(1)}, f32[2,2,8,1280]{3,2,1,0:T(8,128)S(1)}, u32[]{:S(2)}, u32[]{:S(2)}) collective-permute-start(f32[2,2,8,1280]{3,2,1,0:T(8,128)S(1)} %add_multiply_fusion.1), channel_id=1, source_target_pairs={{0,8},{4,12},{8,0},{12,4},{16,24},{20,28},{24,16},{28,20},{1,9},{5... | collective-permute-start | bytes 491528 | tf_op jit(solution)/shard_map/ppermute | solution.py:190
  77.9 4.2 %collective-permute-done.24 = f32[2,2,8,1280]{3,2,1,0:T(8,128)S(1)} collective-permute-done((f32[2,2,8,1280]{3,2,1,0:T(8,128)S(1)}, f32[2,2,8,1280]{3,2,1,0:T(8,128)S(1)}, u32[]{:S(2)}, u32[]{:S(2)}) %collective-permute-start.24) | collective-permute-done | bytes 163872 | tf_op jit(solution)/shard_map/ppermute | solution.py:190
  82.3 3.4 %collective-permute-done.7 = f32[2,2,8,1280]{3,2,1,0:T(8,128)S(1)} collective-permute-done((f32[2,2,8,1280]{3,2,1,0:T(8,128)S(1)}, f32[2,2,8,1280]{3,2,1,0:T(8,128)S(1)}, u32[]{:S(2)}, u32[]{:S(2)}) %collective-permute-start.7) | collective-permute-done | bytes 163872 | tf_op jit(solution)/shard_map/ppermute | solution.py:190
  85.8 3.4 %collective-permute-done.12 = f32[2,2,8,1280]{3,2,1,0:T(8,128)S(1)} collective-permute-done((f32[2,2,8,1280]{3,2,1,0:T(8,128)S(1)}, f32[2,2,8,1280]{3,2,1,0:T(8,128)S(1)}, u32[]{:S(2)}, u32[]{:S(2)}) %collective-permute-start.12) | collective-permute-done | bytes 163872 | tf_op jit(solution)/shard_map/ppermute | solution.py:190
  89.3 3.6 %collective-permute-done.20 = f32[2,2,8,1280]{3,2,1,0:T(8,128)S(1)} collective-permute-done((f32[2,2,8,1280]{3,2,1,0:T(8,128)S(1)}, f32[2,2,8,1280]{3,2,1,0:T(8,128)S(1)}, u32[]{:S(2)}, u32[]{:S(2)}) %collective-permute-start.20) | collective-permute-done | bytes 163872 | tf_op jit(solution)/shard_map/ppermute | solution.py:190
  94.2 2.2 %collective-permute-done.25 = f32[2,2,8,1280]{3,2,1,0:T(8,128)S(1)} collective-permute-done((f32[2,2,8,1280]{3,2,1,0:T(8,128)S(1)}, f32[2,2,8,1280]{3,2,1,0:T(8,128)S(1)}, u32[]{:S(2)}, u32[]{:S(2)}) %collective-permute-start.25) | collective-permute-done | bytes 163872 | tf_op jit(solution)/shard_map/ppermute | solution.py:190
  97.7 2.2 %collective-permute-done.8 = f32[2,2,8,1280]{3,2,1,0:T(8,128)S(1)} collective-permute-done((f32[2,2,8,1280]{3,2,1,0:T(8,128)S(1)}, f32[2,2,8,1280]{3,2,1,0:T(8,128)S(1)}, u32[]{:S(2)}, u32[]{:S(2)}) %collective-permute-start.8) | collective-permute-done | bytes 163872 | tf_op jit(solution)/shard_map/ppermute | solution.py:190
  101.2 2.2 %collective-permute-done.13 = f32[2,2,8,1280]{3,2,1,0:T(8,128)S(1)} collective-permute-done((f32[2,2,8,1280]{3,2,1,0:T(8,128)S(1)}, f32[2,2,8,1280]{3,2,1,0:T(8,128)S(1)}, u32[]{:S(2)}, u32[]{:S(2)}) %collective-permute-start.13) | collective-permute-done | bytes 163872 | tf_op jit(solution)/shard_map/ppermute | solution.py:190
  104.8 2.8 %collective-permute-done.26.refs_3_ = f32[4,2,8,1280]{3,2,1,0:T(8,128)S(1)} collective-permute-done((f32[4,2,8,1280]{3,2,1,0:T(8,128)S(1)}, f32[4,2,8,1280]{3,2,1,0:T(8,128)S(1)}, u32[]{:S(2)}, u32[]{:S(2)}) %collective-permute-start.26) | collective-permute-done | bytes 327712 | tf_op jit(solution)/shard_map/ppermute | solution.py:190
  108.0 4.8 %collective-permute-start.27 = (f32[16,4,1280]{2,1,0:T(4,128)S(1)}, f32[16,4,1280]{2,1,0:T(4,128)S(1)}, u32[]{:S(2)}, u32[]{:S(2)}) collective-permute-start(f32[16,4,1280]{2,1,0:T(4,128)S(1)} %get-tuple-element.44), channel_id=1, source_target_pairs={{0,1},{1,0},{2,3},{3,2},{4,5},{5,4},{6,7},{7,6},{8,9},{9,8},{10,11... | collective-permute-start | bytes 983048 | tf_op jit(solution)/shard_map/ppermute | solution.py:197
  112.8 3.0 %collective-permute-start.28 = (f32[16,4,1280]{2,1,0:T(4,128)S(1)}, f32[16,4,1280]{2,1,0:T(4,128)S(1)}, u32[]{:S(2)}, u32[]{:S(2)}) collective-permute-start(f32[16,4,1280]{2,1,0:T(4,128)S(1)} %get-tuple-element.45), channel_id=1, source_target_pairs={{1,2},{2,1},{5,6},{6,5},{9,10},{10,9},{13,14},{14,13},{17,18},{18,... | collective-permute-start | bytes 983048 | tf_op jit(solution)/shard_map/ppermute | solution.py:198
  116.7 5.0 %collective-permute-done.14.refs_3_ = f32[4,2,8,1280]{3,2,1,0:T(8,128)S(1)} collective-permute-done((f32[4,2,8,1280]{3,2,1,0:T(8,128)S(1)}, f32[4,2,8,1280]{3,2,1,0:T(8,128)S(1)}, u32[]{:S(2)}, u32[]{:S(2)}) %collective-permute-start.14) | collective-permute-done | bytes 327712 | tf_op jit(solution)/shard_map/ppermute | solution.py:190
  122.1 2.6 %collective-permute-start.15 = (f32[16,4,1280]{2,1,0:T(4,128)S(1)}, f32[16,4,1280]{2,1,0:T(4,128)S(1)}, u32[]{:S(2)}, u32[]{:S(2)}) collective-permute-start(f32[16,4,1280]{2,1,0:T(4,128)S(1)} %get-tuple-element.33), channel_id=1, source_target_pairs={{0,1},{1,0},{2,3},{3,2},{4,5},{5,4},{6,7},{7,6},{8,9},{9,8},{10,11... | collective-permute-start | bytes 983048 | tf_op jit(solution)/shard_map/ppermute | solution.py:197
  124.7 3.0 %collective-permute-start.16 = (f32[16,4,1280]{2,1,0:T(4,128)S(1)}, f32[16,4,1280]{2,1,0:T(4,128)S(1)}, u32[]{:S(2)}, u32[]{:S(2)}) collective-permute-start(f32[16,4,1280]{2,1,0:T(4,128)S(1)} %get-tuple-element.34), channel_id=1, source_target_pairs={{1,2},{2,1},{5,6},{6,5},{9,10},{10,9},{13,14},{14,13},{17,18},{18,... | collective-permute-start | bytes 983048 | tf_op jit(solution)/shard_map/ppermute | solution.py:198
  128.0 5.9 %shard_map.81.refs_0_ = f32[2,16,8,1280]{3,2,1,0:T(8,128)} custom-call(f32[2,16,8,1280]{3,2,1,0:T(8,128)S(1)} %copy-done.1, f32[2,8,8,1280]{3,2,1,0:T(8,128)S(1)} %get-tuple-element.43.back, f32[16,8,1280]{2,1,0:T(8,128)S(1)} %pad_maximum_fusion.3.beyond, f32[8,1280]{1,0:T(8,128)S(1)} %fusion.14.k_beyond, f32[8,1280]{1,0:T(8,128)S(1)} %copy-done.2), custom_call_target="tpu_custom_call" | custom-call | tf_op jit(solution)/shard_map/pallas_call | solution.py:281
  134.1 5.9 %shard_map.82 = f32[2,16,8,1280]{3,2,1,0:T(8,128)} custom-call(f32[2,16,8,1280]{3,2,1,0:T(8,128)S(1)} %copy-done.1, f32[2,8,8,1280]{3,2,1,0:T(8,128)S(1)} %get-tuple-element.32.back, f32[16,8,1280]{2,1,0:T(8,128)S(1)} %pad_maximum_fusion.2.beyond, f32[8,1280]{1,0:T(8,128)S(1)} %fusion.14.k_beyond, ...), custom_call_target="tpu_custom_call", output_to_operand_aliasing={{}: (5, {})} | custom-call | tf_op jit(solution)/shard_map/pallas_call | solution.py:281
  (98 shorter events, 18.9 us)
Async XLA Ops:
  1.6 17.6 %collective-permute-start = (f32[4,2,8,1280]{3,2,0,1:T(8,128)S(1)}, f32[4,2,8,1280]{3,2,0,1:T(8,128)S(1)}, u32[]{:S(2)}, u32[]{:S(2)}) collective-permute-start(f32[4,2,8,1280]{3,2,0,1:T(8,128)S(1)} %copy.10), channel_id=1, source_target_pairs={{0,16},{4,20},{8,24},{12,28},{16,0},{20,4},{24,8},{28,12},{1,17},{... | collective-permute-start | bytes 983048 | tf_op jit(solution)/shard_map/ppermute | solution.py:190
  6.2 4.2 %copy-start.2 = (f32[8,1280]{1,0:T(8,128)S(1)}, f32[8,1280]{1,0:T(8,128)}, u32[]{:S(2)}) copy-start(f32[8,1280]{1,0:T(8,128)} %kappa.7) | copy-start | bytes 122884
  6.2 6.9 %copy-start.4 = (f32[4,2,8,1280]{3,2,1,0:T(8,128)S(1)}, f32[4,2,8,1280]{3,2,1,0:T(8,128)}, u32[]{:S(2)}) copy-start(f32[4,2,8,1280]{3,2,1,0:T(8,128)} %param.10) | copy-start | bytes 983044
  6.4 6.8 %copy-start.5 = (f32[4,2,8,1280]{3,2,1,0:T(8,128)S(1)}, f32[4,2,8,1280]{3,2,1,0:T(8,128)}, u32[]{:S(2)}) copy-start(f32[4,2,8,1280]{3,2,1,0:T(8,128)} %param.11) | copy-start | bytes 983044
  6.4 6.9 %collective-permute-start.1 = (f32[16,4,1280]{2,1,0:T(4,128)S(1)}, f32[16,4,1280]{2,1,0:T(4,128)S(1)}, u32[]{:S(2)}, u32[]{:S(2)}) collective-permute-start(f32[16,4,1280]{2,1,0:T(4,128)S(1)} %get-tuple-element.60), channel_id=1, source_target_pairs={{0,1},{1,0},{2,3},{3,2},{4,5},{5,4},{6,7},{7,6},{8,9},{9,8},{10,11... | collective-permute-start | bytes 983048 | tf_op jit(solution)/shard_map/ppermute | solution.py:197
  7.4 8.7 %collective-permute-start.2 = (f32[16,4,1280]{2,1,0:T(4,128)S(1)}, f32[16,4,1280]{2,1,0:T(4,128)S(1)}, u32[]{:S(2)}, u32[]{:S(2)}) collective-permute-start(f32[16,4,1280]{2,1,0:T(4,128)S(1)} %get-tuple-element.61), channel_id=1, source_target_pairs={{1,2},{2,1},{5,6},{6,5},{9,10},{10,9},{13,14},{14,13},{17,18},{18,... | collective-permute-start | bytes 983048 | tf_op jit(solution)/shard_map/ppermute | solution.py:198
  10.6 8.8 %collective-permute-start.3 = (f32[17,4,1280]{2,1,0:T(4,128)S(1)}, f32[17,4,1280]{2,1,0:T(4,128)S(1)}, u32[]{:S(2)}, u32[]{:S(2)}) collective-permute-start(f32[17,4,1280]{2,1,0:T(4,128)S(1)} %get-tuple-element.52), channel_id=1, source_target_pairs={{0,1},{1,0},{2,3},{3,2},{4,5},{5,4},{6,7},{7,6},{8,9},{9,8},{10,11... | collective-permute-start | bytes 1044488 | tf_op jit(solution)/shard_map/ppermute | solution.py:197
  10.6 9.1 %collective-permute-start.4 = (f32[17,4,1280]{2,1,0:T(4,128)S(1)}, f32[17,4,1280]{2,1,0:T(4,128)S(1)}, u32[]{:S(2)}, u32[]{:S(2)}) collective-permute-start(f32[17,4,1280]{2,1,0:T(4,128)S(1)} %get-tuple-element.53), channel_id=1, source_target_pairs={{1,2},{2,1},{5,6},{6,5},{9,10},{10,9},{13,14},{14,13},{17,18},{18,... | collective-permute-start | bytes 1044488 | tf_op jit(solution)/shard_map/ppermute | solution.py:198
  27.0 8.6 %collective-permute-start.17 = (f32[4,2,8,1280]{3,2,1,0:T(8,128)S(1)}, f32[4,2,8,1280]{3,2,1,0:T(8,128)S(1)}, u32[]{:S(2)}, u32[]{:S(2)}) collective-permute-start(f32[4,2,8,1280]{3,2,1,0:T(8,128)S(1)} %get-tuple-element.37), channel_id=1, source_target_pairs={{0,4},{4,0},{8,12},{12,8},{16,20},{20,16},{24,28},{28,24},{1,5},{5... | collective-permute-start | bytes 983048 | tf_op jit(solution)/shard_map/ppermute | solution.py:190
  28.4 13.8 %collective-permute-start.22 = (f32[4,2,8,1280]{3,2,1,0:T(8,128)S(1)}, f32[4,2,8,1280]{3,2,1,0:T(8,128)S(1)}, u32[]{:S(2)}, u32[]{:S(2)}) collective-permute-start(f32[4,2,8,1280]{3,2,1,0:T(8,128)S(1)} %get-tuple-element.41), channel_id=1, source_target_pairs={{0,4},{4,0},{8,12},{12,8},{16,20},{20,16},{24,28},{28,24},{1,5},{5... | collective-permute-start | bytes 983048 | tf_op jit(solution)/shard_map/ppermute | solution.py:190
  34.1 15.2 %collective-permute-start.5 = (f32[4,2,8,1280]{3,2,1,0:T(8,128)S(1)}, f32[4,2,8,1280]{3,2,1,0:T(8,128)S(1)}, u32[]{:S(2)}, u32[]{:S(2)}) collective-permute-start(f32[4,2,8,1280]{3,2,1,0:T(8,128)S(1)} %get-tuple-element.26), channel_id=1, source_target_pairs={{0,4},{4,0},{8,12},{12,8},{16,20},{20,16},{24,28},{28,24},{1,5},{5... | collective-permute-start | bytes 983048 | tf_op jit(solution)/shard_map/ppermute | solution.py:190
  35.4 21.0 %collective-permute-start.10 = (f32[4,2,8,1280]{3,2,1,0:T(8,128)S(1)}, f32[4,2,8,1280]{3,2,1,0:T(8,128)S(1)}, u32[]{:S(2)}, u32[]{:S(2)}) collective-permute-start(f32[4,2,8,1280]{3,2,1,0:T(8,128)S(1)} %get-tuple-element.30), channel_id=1, source_target_pairs={{0,4},{4,0},{8,12},{12,8},{16,20},{20,16},{24,28},{28,24},{1,5},{5... | collective-permute-start | bytes 983048 | tf_op jit(solution)/shard_map/ppermute | solution.py:190
  35.6 22.5 %collective-permute-start.18 = (f32[2,2,8,1280]{3,2,1,0:T(8,128)S(1)}, f32[2,2,8,1280]{3,2,1,0:T(8,128)S(1)}, u32[]{:S(2)}, u32[]{:S(2)}) collective-permute-start(f32[2,2,8,1280]{3,2,1,0:T(8,128)S(1)} %slice_add_fusion.2), channel_id=1, source_target_pairs={{0,8},{4,12},{8,0},{12,4},{16,24},{20,28},{24,16},{28,20},{1,9},{5... | collective-permute-start | bytes 491528 | tf_op jit(solution)/shard_map/ppermute | solution.py:190
  42.3 19.0 %collective-permute-start.23 = (f32[2,2,8,1280]{3,2,1,0:T(8,128)S(1)}, f32[2,2,8,1280]{3,2,1,0:T(8,128)S(1)}, u32[]{:S(2)}, u32[]{:S(2)}) collective-permute-start(f32[2,2,8,1280]{3,2,1,0:T(8,128)S(1)} %slice_add_fusion), channel_id=1, source_target_pairs={{0,8},{4,12},{8,0},{12,4},{16,24},{20,28},{24,16},{28,20},{1,9},{5... | collective-permute-start | bytes 491528 | tf_op jit(solution)/shard_map/ppermute | solution.py:190
  49.3 12.1 %collective-permute-start.6 = (f32[2,2,8,1280]{3,2,1,0:T(8,128)S(1)}, f32[2,2,8,1280]{3,2,1,0:T(8,128)S(1)}, u32[]{:S(2)}, u32[]{:S(2)}) collective-permute-start(f32[2,2,8,1280]{3,2,1,0:T(8,128)S(1)} %slice_add_fusion.6), channel_id=1, source_target_pairs={{0,8},{4,12},{8,0},{12,4},{16,24},{20,28},{24,16},{28,20},{1,9},{5... | collective-permute-start | bytes 491528 | tf_op jit(solution)/shard_map/ppermute | solution.py:190
  56.3 7.6 %collective-permute-start.11 = (f32[2,2,8,1280]{3,2,1,0:T(8,128)S(1)}, f32[2,2,8,1280]{3,2,1,0:T(8,128)S(1)}, u32[]{:S(2)}, u32[]{:S(2)}) collective-permute-start(f32[2,2,8,1280]{3,2,1,0:T(8,128)S(1)} %slice_add_fusion.4), channel_id=1, source_target_pairs={{0,8},{4,12},{8,0},{12,4},{16,24},{20,28},{24,16},{28,20},{1,9},{5... | collective-permute-start | bytes 491528 | tf_op jit(solution)/shard_map/ppermute | solution.py:190
  58.2 7.5 %collective-permute-start.19 = (f32[2,2,8,1280]{3,2,1,0:T(8,128)S(1)}, f32[2,2,8,1280]{3,2,1,0:T(8,128)S(1)}, u32[]{:S(2)}, u32[]{:S(2)}) collective-permute-start(f32[2,2,8,1280]{3,2,1,0:T(8,128)S(1)} %pad_maximum_fusion.16), channel_id=1, source_target_pairs={{0,16},{4,20},{8,24},{12,28},{16,0},{20,4},{24,8},{28,12},{1,17},{... | collective-permute-start | bytes 491528 | tf_op jit(solution)/shard_map/ppermute | solution.py:190
  61.3 20.8 %collective-permute-start.24 = (f32[2,2,8,1280]{3,2,1,0:T(8,128)S(1)}, f32[2,2,8,1280]{3,2,1,0:T(8,128)S(1)}, u32[]{:S(2)}, u32[]{:S(2)}) collective-permute-start(f32[2,2,8,1280]{3,2,1,0:T(8,128)S(1)} %pad_maximum_fusion.17), channel_id=1, source_target_pairs={{0,16},{4,20},{8,24},{12,28},{16,0},{20,4},{24,8},{28,12},{1,17},{... | collective-permute-start | bytes 491528 | tf_op jit(solution)/shard_map/ppermute | solution.py:190
  61.5 24.1 %collective-permute-start.7 = (f32[2,2,8,1280]{3,2,1,0:T(8,128)S(1)}, f32[2,2,8,1280]{3,2,1,0:T(8,128)S(1)}, u32[]{:S(2)}, u32[]{:S(2)}) collective-permute-start(f32[2,2,8,1280]{3,2,1,0:T(8,128)S(1)} %pad_maximum_fusion.14), channel_id=1, source_target_pairs={{0,16},{4,20},{8,24},{12,28},{16,0},{20,4},{24,8},{28,12},{1,17},{... | collective-permute-start | bytes 491528 | tf_op jit(solution)/shard_map/ppermute | solution.py:190
  64.0 25.1 %collective-permute-start.12 = (f32[2,2,8,1280]{3,2,1,0:T(8,128)S(1)}, f32[2,2,8,1280]{3,2,1,0:T(8,128)S(1)}, u32[]{:S(2)}, u32[]{:S(2)}) collective-permute-start(f32[2,2,8,1280]{3,2,1,0:T(8,128)S(1)} %pad_maximum_fusion.15), channel_id=1, source_target_pairs={{0,16},{4,20},{8,24},{12,28},{16,0},{20,4},{24,8},{28,12},{1,17},{... | collective-permute-start | bytes 491528 | tf_op jit(solution)/shard_map/ppermute | solution.py:190
  65.7 27.2 %collective-permute-start.20 = (f32[2,2,8,1280]{3,2,1,0:T(8,128)S(1)}, f32[2,2,8,1280]{3,2,1,0:T(8,128)S(1)}, u32[]{:S(2)}, u32[]{:S(2)}) collective-permute-start(f32[2,2,8,1280]{3,2,1,0:T(8,128)S(1)} %add_multiply_fusion.1), channel_id=1, source_target_pairs={{0,8},{4,12},{8,0},{12,4},{16,24},{20,28},{24,16},{28,20},{1,9},{5... | collective-permute-start | bytes 491528 | tf_op jit(solution)/shard_map/ppermute | solution.py:190
  82.2 14.3 %collective-permute-start.25 = (f32[2,2,8,1280]{3,2,1,0:T(8,128)S(1)}, f32[2,2,8,1280]{3,2,1,0:T(8,128)S(1)}, u32[]{:S(2)}, u32[]{:S(2)}) collective-permute-start(f32[2,2,8,1280]{3,2,1,0:T(8,128)S(1)} %add_multiply_fusion), channel_id=1, source_target_pairs={{0,8},{4,12},{8,0},{12,4},{16,24},{20,28},{24,16},{28,20},{1,9},{5... | collective-permute-start | bytes 491528 | tf_op jit(solution)/shard_map/ppermute | solution.py:190
  85.7 14.3 %collective-permute-start.8 = (f32[2,2,8,1280]{3,2,1,0:T(8,128)S(1)}, f32[2,2,8,1280]{3,2,1,0:T(8,128)S(1)}, u32[]{:S(2)}, u32[]{:S(2)}) collective-permute-start(f32[2,2,8,1280]{3,2,1,0:T(8,128)S(1)} %add_multiply_fusion.3), channel_id=1, source_target_pairs={{0,8},{4,12},{8,0},{12,4},{16,24},{20,28},{24,16},{28,20},{1,9},{5... | collective-permute-start | bytes 491528 | tf_op jit(solution)/shard_map/ppermute | solution.py:190
  89.2 14.3 %collective-permute-start.13 = (f32[2,2,8,1280]{3,2,1,0:T(8,128)S(1)}, f32[2,2,8,1280]{3,2,1,0:T(8,128)S(1)}, u32[]{:S(2)}, u32[]{:S(2)}) collective-permute-start(f32[2,2,8,1280]{3,2,1,0:T(8,128)S(1)} %add_multiply_fusion.2), channel_id=1, source_target_pairs={{0,8},{4,12},{8,0},{12,4},{16,24},{20,28},{24,16},{28,20},{1,9},{5... | collective-permute-start | bytes 491528 | tf_op jit(solution)/shard_map/ppermute | solution.py:190
  93.0 11.8 %collective-permute-start.21 = (f32[4,2,8,1280]{3,2,1,0:T(8,128)S(1)}, f32[4,2,8,1280]{3,2,1,0:T(8,128)S(1)}, u32[]{:S(2)}, u32[]{:S(2)}) collective-permute-start(f32[4,2,8,1280]{3,2,1,0:T(8,128)S(1)} %pad_maximum_fusion.7.refs_0_), channel_id=1, source_target_pairs={{0,4},{4,0},{8,12},{12,8},{16,20},{20,16},{24,28},{28,24},{1,5},{5... | collective-permute-start | bytes 983048 | tf_op jit(solution)/shard_map/ppermute | solution.py:190
  96.5 11.1 %collective-permute-start.26 = (f32[4,2,8,1280]{3,2,1,0:T(8,128)S(1)}, f32[4,2,8,1280]{3,2,1,0:T(8,128)S(1)}, u32[]{:S(2)}, u32[]{:S(2)}) collective-permute-start(f32[4,2,8,1280]{3,2,1,0:T(8,128)S(1)} %pad_maximum_fusion.8.refs_2_), channel_id=1, source_target_pairs={{0,4},{4,0},{8,12},{12,8},{16,20},{20,16},{24,28},{28,24},{1,5},{5... | collective-permute-start | bytes 983048 | tf_op jit(solution)/shard_map/ppermute | solution.py:190
  100.0 16.7 %collective-permute-start.9 = (f32[4,2,8,1280]{3,2,1,0:T(8,128)S(1)}, f32[4,2,8,1280]{3,2,1,0:T(8,128)S(1)}, u32[]{:S(2)}, u32[]{:S(2)}) collective-permute-start(f32[4,2,8,1280]{3,2,1,0:T(8,128)S(1)} %pad_maximum_fusion.5.refs_0_), channel_id=1, source_target_pairs={{0,4},{4,0},{8,12},{12,8},{16,20},{20,16},{24,28},{28,24},{1,5},{5... | collective-permute-start | bytes 983048 | tf_op jit(solution)/shard_map/ppermute | solution.py:190
  103.5 18.2 %collective-permute-start.14 = (f32[4,2,8,1280]{3,2,1,0:T(8,128)S(1)}, f32[4,2,8,1280]{3,2,1,0:T(8,128)S(1)}, u32[]{:S(2)}, u32[]{:S(2)}) collective-permute-start(f32[4,2,8,1280]{3,2,1,0:T(8,128)S(1)} %pad_maximum_fusion.6.refs_2_), channel_id=1, source_target_pairs={{0,4},{4,0},{8,12},{12,8},{16,20},{20,16},{24,28},{28,24},{1,5},{5... | collective-permute-start | bytes 983048 | tf_op jit(solution)/shard_map/ppermute | solution.py:190
  108.0 19.7 %collective-permute-start.27 = (f32[16,4,1280]{2,1,0:T(4,128)S(1)}, f32[16,4,1280]{2,1,0:T(4,128)S(1)}, u32[]{:S(2)}, u32[]{:S(2)}) collective-permute-start(f32[16,4,1280]{2,1,0:T(4,128)S(1)} %get-tuple-element.44), channel_id=1, source_target_pairs={{0,1},{1,0},{2,3},{3,2},{4,5},{5,4},{6,7},{7,6},{8,9},{9,8},{10,11... | collective-permute-start | bytes 983048 | tf_op jit(solution)/shard_map/ppermute | solution.py:197
  112.8 14.9 %collective-permute-start.28 = (f32[16,4,1280]{2,1,0:T(4,128)S(1)}, f32[16,4,1280]{2,1,0:T(4,128)S(1)}, u32[]{:S(2)}, u32[]{:S(2)}) collective-permute-start(f32[16,4,1280]{2,1,0:T(4,128)S(1)} %get-tuple-element.45), channel_id=1, source_target_pairs={{1,2},{2,1},{5,6},{6,5},{9,10},{10,9},{13,14},{14,13},{17,18},{18,... | collective-permute-start | bytes 983048 | tf_op jit(solution)/shard_map/ppermute | solution.py:198
  122.1 11.8 %collective-permute-start.15 = (f32[16,4,1280]{2,1,0:T(4,128)S(1)}, f32[16,4,1280]{2,1,0:T(4,128)S(1)}, u32[]{:S(2)}, u32[]{:S(2)}) collective-permute-start(f32[16,4,1280]{2,1,0:T(4,128)S(1)} %get-tuple-element.33), channel_id=1, source_target_pairs={{0,1},{1,0},{2,3},{3,2},{4,5},{5,4},{6,7},{7,6},{8,9},{9,8},{10,11... | collective-permute-start | bytes 983048 | tf_op jit(solution)/shard_map/ppermute | solution.py:197
  124.7 9.2 %collective-permute-start.16 = (f32[16,4,1280]{2,1,0:T(4,128)S(1)}, f32[16,4,1280]{2,1,0:T(4,128)S(1)}, u32[]{:S(2)}, u32[]{:S(2)}) collective-permute-start(f32[16,4,1280]{2,1,0:T(4,128)S(1)} %get-tuple-element.34), channel_id=1, source_target_pairs={{1,2},{2,1},{5,6},{6,5},{9,10},{10,9},{13,14},{14,13},{17,18},{18,... | collective-permute-start | bytes 983048 | tf_op jit(solution)/shard_map/ppermute | solution.py:198
  (3 other events, 4.9 us)
where the time goes:
time: 140 us
  starting transfers between devices  57.9 us (41%)
  waiting for transfers between devices  51.1 us (36%)
  Pallas kernels  23.2 us (17%)
  local copies, waits for them, and re-layouts  4.82 us (3%)
  other arithmetic  1.73 us (1%)
    ppermute x21, waiting for transfers between devices, exchange(): return lax.ppermute(x, 'member', [(i, i ^ bit) for i in range(count)])  47.9 us
    ppermute x21, starting transfers between devices, exchange(): return lax.ppermute(x, 'member', [(i, i ^ bit) for i in range(count)])  37.7 us
    pallas_call x2, Pallas kernels, inner(): pl.pallas_call(functools.partial(adjoint_kernel, c, width), out_shape=jax...  11.8 us
    ppermute x4, starting transfers between devices, halves(): far = lax.ppermute(to_next, 'space', nexts)  11.6 us
    pallas_call x4, Pallas kernels, call(): pl.pallas_call(kernel, out_shape=[jax.ShapeDtypeStruct(shape, F32) for sh...  11.5 us
    ppermute x4, starting transfers between devices, halves(): near = lax.ppermute(to_partner, 'space', pairs)  8.51 us
    unnamed x14, local copies, waits for them, and re-layouts  3.31 us
    ppermute x4, waiting for transfers between devices, halves(): far = lax.ppermute(to_next, 'space', nexts)  3.26 us
  transfers between devices with their start and end apart: 29, of which 15 were waited for; matrix products, arithmetic and copies ran while one was open for 3% of the time, Pallas kernels for 9%

commit v1 on v0

--- a/solution.py
+++ b/solution.py
@@ -12,40 +12,58 @@
 F32 = jnp.float32
 
 
-def fill_faces(faces, kappa, beyond):
+OWN, BEYOND = pl.ds(0, 8), pl.ds(8, 8)
+EVEN, ODD = pl.ds(0, 8, stride=2), pl.ds(1, 8, stride=2)
+LANES = 128
+
+
+def put(pair, rows, value):
+    for j in range(pair.shape[0]):
+        pair[j, rows, :] = value[:, j * LANES : (j + 1) * LANES]
+
+
+def get(pair, rows):
+    return jnp.concatenate([pair[j, rows, :] for j in range(pair.shape[0])], axis=1)
+
+
+def fill_faces(faces, pair, kappa, beyond):
     width = kappa.shape[-1]
+    put(pair, OWN, kappa)
+    put(pair, BEYOND, beyond)
+    even, odd = get(pair, EVEN), get(pair, ODD)
     row = lax.broadcasted_iota(jnp.int32, kappa.shape, 0)
-    last = row == kappa.shape[0] - 1
-    here, there = pltpu.roll(kappa, 7, 0), pltpu.roll(beyond, 7, 0)
-    faces[0] = 0.5 * (kappa + pltpu.roll(kappa, width - 1, 1))
-    faces[1] = 0.5 * (beyond + pltpu.roll(beyond, width - 1, 1))
-    faces[2] = 0.5 * (kappa + jnp.where(last, there, here))
-    faces[3] = 0.5 * (beyond + jnp.where(last, here, there))
     place, count = lax.axis_index("space"), lax.axis_size("space")
     has_above = (place < count - 1).astype(F32)
     has_below = (place > 0).astype(F32)
-    faces[4] = jnp.where(row < 4, has_above, has_below)
-
-
-def diffuse(faces, u, h):
+    inside = jnp.where(row < 4, 1.0, jnp.where(row < 6, has_above, has_below))
+    for at, tile, north, south in (
+        (0, even, odd, pltpu.roll(odd, 1, 0)),
+        (5, odd, pltpu.roll(even, 7, 0), even),
+    ):
+        shares = [
+            0.5 * (tile + near)
+            for near in (pltpu.roll(tile, width - 1, 1), pltpu.roll(tile, 1, 1), north, south)
+        ]
+        faces[at] = inside * (1.0 - ((shares[0] + shares[1]) + (shares[2] + shares[3])))
+        for k, share in enumerate(shares):
+            faces[at + 1 + k] = inside * share
+
+
+def diffuse(faces, pair, u, h):
     width = u.shape[-1]
-    row = lax.broadcasted_iota(jnp.int32, u.shape, 0)
-    last, first = row == u.shape[0] - 1, row == 0
-
-    def along(v, face):
-        flux = face * (pltpu.roll(v, width - 1, 1) - v)
-        return flux - pltpu.roll(flux, 1, 1)
-
-    for sweep in range(STEPS):
-        ru, rh = pltpu.roll(u, 7, 0), pltpu.roll(h, 7, 0)
-        fu = faces[2] * (jnp.where(last, rh, ru) - u)
-        fh = faces[3] * (jnp.where(last, ru, rh) - h)
-        su, sh = pltpu.roll(fu, 1, 0), pltpu.roll(fh, 1, 0)
-        v = u + along(u, faces[0]) + (fu - jnp.where(first, sh, su))
-        if sweep < STEPS - 1:
-            h = faces[4] * (h + along(h, faces[1]) + (fh - jnp.where(first, su, sh)))
-        u = v
-    return u
+
+    def step(at, tile, north, south):
+        lateral = faces[at + 1] * pltpu.roll(tile, width - 1, 1) + faces[at + 2] * pltpu.roll(tile, 1, 1)
+        return (faces[at] * tile + lateral) + (faces[at + 3] * north + faces[at + 4] * south)
+
+    put(pair, OWN, u)
+    put(pair, BEYOND, h)
+    even, odd = get(pair, EVEN), get(pair, ODD)
+    for _ in range(STEPS):
+        even, odd = step(0, even, odd, pltpu.roll(odd, 1, 0)), step(5, odd, pltpu.roll(even, 7, 0), even)
+    put(pair, EVEN, even)
+    put(pair, ODD, odd)
+    return get(pair, OWN)
 
 
 def place_of(index, bits):
@@ -62,12 +80,31 @@
     return index
 
 
+def edges_kernel(width, alpha, kappa, perturb, *outs):
+    members = alpha.shape[0]
+    count = alpha.shape[1] // width
+    even = lax.rem(lax.axis_index("space"), 2) == 0
+
+    def send(chunk, at, rows):
+        outs[2 * chunk][at] = jnp.where(even, rows[4:], rows[:4])
+        outs[2 * chunk + 1][at] = jnp.where(even, rows[:4], rows[4:])
+
+    def level(piece, carry):
+        for chunk in range(width):
+            for m in range(members):
+                send(chunk, m * count + piece, alpha[m, piece * width + chunk])
+        return carry
+
+    lax.fori_loop(0, count, level, 0)
+    send(0, members * count, kappa[...])
+
+
 def forward_kernel(chunk, width, groups, alpha, beyond, k_beyond, kappa, land, perturb, *refs):
-    faces, outs = refs[-1], refs[:-1]
+    faces, pair, outs = refs[-2], refs[-1], refs[:-2]
     members = perturb.shape[1]
     count = 2 * outs[0].shape[0]
     me = lax.axis_index("member")
-    fill_faces(faces, kappa[...], k_beyond[...])
+    fill_faces(faces, pair.at[0], kappa[...], k_beyond[...])
     lead = groups[0][1]
     for half in (1, 0):
         def level(i, carry, half=half):
@@ -76,7 +113,7 @@
             row = piece * width + chunk
             local = []
             for m in range(members):
-                local.append(diffuse(faces, alpha[m, row], beyond[m * count + piece]) * land[...].astype(F32))
+                local.append(diffuse(faces, pair.at[m], alpha[m, row], beyond[m * count + piece]) * land[...].astype(F32))
 
             def added(t):
                 total = perturb[t, 0, row].astype(F32) * local[0]
@@ -145,9 +182,9 @@
 
 
 def adjoint_kernel(chunk, width, alpha, back, beyond, k_beyond, kappa, *refs):
-    gradient, faces, stage, done = refs[-4:]
+    gradient, faces, pair, stage, done = refs[-5:]
     members, count = back.shape[:2]
-    fill_faces(faces, kappa[...], k_beyond[...])
+    fill_faces(faces, pair.at[0], kappa[...], k_beyond[...])
 
     def copy(m, piece):
         return pltpu.make_async_copy(
@@ -156,7 +193,7 @@
 
     def level(piece, carry):
         for m in range(members):
-            value = diffuse(faces, back[m, piece], beyond[m * count + piece])
+            value = diffuse(faces, pair.at[m], back[m, piece], beyond[m * count + piece])
             stage[m, piece] = value + alpha[m, piece * width + chunk]
             copy(m, piece).start()
         return carry
@@ -190,12 +227,18 @@
     return lax.ppermute(x, "member", [(i, i ^ bit) for i in range(count)])
 
 
+def to_partner_chip(x):
+    ends = lax.axis_size("space")
+    return lax.ppermute(x, "space", [(i, i ^ 1) for i in range(ends)])
+
+
+def to_next_chip(x):
+    ends = lax.axis_size("space")
+    return lax.ppermute(x, "space", [(i, i + 1 if i % 2 else i - 1) for i in range(1, ends - 1)])
+
+
 def halves(to_partner, to_next):
-    ends = lax.axis_size("space")
-    pairs = [(i, i ^ 1) for i in range(ends)]
-    nexts = [(i, i + 1 if i % 2 else i - 1) for i in range(1, ends - 1)]
-    near = lax.ppermute(to_partner, "space", pairs)
-    far = lax.ppermute(to_next, "space", nexts)
+    near, far = to_partner_chip(to_partner), to_next_chip(to_next)
     even = lax.rem(lax.axis_index("space"), 2) == 0
     return jnp.concatenate([jnp.where(even, near, far), jnp.where(even, far, near)], axis=1)
 
@@ -223,18 +266,14 @@
     count = lax.axis_size("member")
     width = obs_weight.shape[1]
     bits = [1 << k for k in range(count.bit_length() - 1)]
+    swapped = [bits[1], bits[0]] + bits[2:]
     early, late = tuple(range(slots // 2)), tuple(range(slots // 2, slots))
-    plans = [((early, bits), (late, bits)) for _ in range(width)]
-
-    even = lax.rem(lax.axis_index("space"), 2) == 0
-    split = alpha.reshape(members, count, width, rows, lon)
-    beyond = []
-    for c in range(width):
-        mine = split[:, :, c].reshape(members * count, rows, lon)
-        if c == 0:
-            mine = jnp.concatenate([mine, kappa[None]], axis=0)
-        low, high = mine[:, :4], mine[:, 4:]
-        beyond.append(halves(jnp.where(even, high, low), jnp.where(even, low, high)))
+    plans = [((early, bits), (late, bits)) for _ in range(width - 1)]
+    plans.append(((early, bits), (late, swapped)))
+
+    shapes = [(members * count + (c == 0), 4, lon) for c in range(width) for _ in range(2)]
+    edges = call(functools.partial(edges_kernel, width), (alpha, kappa, perturb), shapes)
+    beyond = [halves(edges[2 * c], edges[2 * c + 1]) for c in range(width)]
     k_beyond = beyond[0][-1]
 
     far_weight = exchange(obs_weight, bits[-1])
@@ -254,7 +293,7 @@
             functools.partial(forward_kernel, c, width, plans[c]),
             (alpha, beyond[c], k_beyond, kappa, land, perturb),
             shapes,
-            [(5, rows, lon)],
+            [(10, rows, lon), (members, lon // LANES, 2 * rows, LANES)],
         )
         for g, (group, order) in enumerate(plans[c]):
             offset, weights = apart[c, g]
@@ -284,7 +323,8 @@
             in_specs=specs,
             out_specs=pl.BlockSpec(memory_space=pl.ANY),
             scratch_shapes=[
-                pltpu.VMEM((5, rows, lon), F32),
+                pltpu.VMEM((10, rows, lon), F32),
+                pltpu.VMEM((members, lon // LANES, 2 * rows, LANES), F32),
                 pltpu.VMEM((members, count, rows, lon), F32),
                 pltpu.SemaphoreType.DMA((members, count)),
             ],

time: 140 us -> 129 us (0.921)
  starting transfers between devices: 57.9 us -> 33 us
  waiting for transfers between devices: 51.1 us -> 61.8 us
  local copies, waits for them, and re-layouts: 4.82 us -> 7.09 us
    ppermute x21, starting transfers between devices: 37.7 us -> 18.5 us  [exchange(): return lax.ppermute(x, 'member', [(i, i ^ bit) for i in range(count)])]
    ppermute x21, waiting for transfers between devices: 47.9 us -> 56.1 us  [exchange(): return lax.ppermute(x, 'member', [(i, i ^ bit) for i in range(count)])]
    ppermute x8, starting transfers between devices: 20.1 us -> 14.5 us  [the longest x4 9.37 us: to_next_chip(): lax.ppermute(x, 'space', [(i, i + 1 if i % 2 else i - 1) for i in range(1...]
    unnamed x14 -> x20, local copies, waits for them, and re-layouts: 3.31 us -> 6.97 us
    ppermute x8, waiting for transfers between devices: 3.27 us -> 5.66 us  [the longest x4 5.65 us: to_next_chip(): lax.ppermute(x, 'space', [(i, i + 1 if i % 2 else i - 1) for i in range(1...]
    pallas_call x4 -> x5, Pallas kernels: 11.5 us -> 11.3 us  [call(): pl.pallas_call(kernel, out_shape=[jax.ShapeDtypeStruct(shape, F32) for sh...]
  transfers between devices with their start and end apart: 29 -> 29, of which waited for: 15 -> 18; matrix products, arithmetic and copies ran while one was open for 3% -> 2% of each run, Pallas kernels for 9% -> 9%
where the time goes in v1:
time: 129 us; the launch traced here: 128 us
  waiting for transfers between devices  61.8 us (48%)
  starting transfers between devices  33 us (26%)
  Pallas kernels  22.8 us (18%)
  local copies, waits for them, and re-layouts  7.09 us (5%)
  other arithmetic  2.59 us (2%)
    ppermute x21, waiting for transfers between devices, exchange(): return lax.ppermute(x, 'member', [(i, i ^ bit) for i in range(count)])  56.1 us
    ppermute x21, starting transfers between devices, exchange(): return lax.ppermute(x, 'member', [(i, i ^ bit) for i in range(count)])  18.5 us
    pallas_call x2, Pallas kernels, inner(): pl.pallas_call(functools.partial(adjoint_kernel, c, width), out_shape=jax...  11.5 us
    pallas_call x5, Pallas kernels, call(): pl.pallas_call(kernel, out_shape=[jax.ShapeDtypeStruct(shape, F32) for sh...  11.3 us
    ppermute x4, starting transfers between devices, to_next_chip(): lax.ppermute(x, 'space', [(i, i + 1 if i % 2 else i - 1) for i in range(1...  9.37 us
    unnamed x20, local copies, waits for them, and re-layouts  6.97 us
    ppermute x4, waiting for transfers between devices, to_next_chip(): lax.ppermute(x, 'space', [(i, i + 1 if i % 2 else i - 1) for i in range(1...  5.65 us
    ppermute x4, starting transfers between devices, to_partner_chip(): return lax.ppermute(x, 'space', [(i, i ^ 1) for i in range(ends)])  5.15 us
  transfers between devices with their start and end apart: 29, of which 18 were waited for; matrix products, arithmetic and copies ran while one was open for 2% of the time, Pallas kernels for 9%

profile of v1, /device:TPU:1, one launch (start us, length us, event | category | flops | bytes accessed | tf_op | source)
XLA Modules:
  0.0 128.3 jit_solution(2955541335196441533)
XLA Ops:
  1.6 3.2 %collective-permute-start = (f32[4,2,8,1280]{3,2,0,1:T(8,128)S(1)}, f32[4,2,8,1280]{3,2,0,1:T(8,128)S(1)}, u32[]{:S(2)}, u32[]{:S(2)}) collective-permute-start(f32[4,2,8,1280]{3,2,0,1:T(8,128)S(1)} %copy.10), channel_id=1, source_target_pairs={{0,16},{4,20},{8,24},{12,28},{16,0},{20,4},{24,8},{28,12},{1,17},{... | collective-permute-start | bytes 983048 | tf_op jit(solution)/shard_map/ppermute | solution.py:227
  4.8 1.7 %copy-done = bf16[4,2,16,8,1280]{4,3,2,1,0:T(8,128)(2,1)S(1)} copy-done((bf16[4,2,16,8,1280]{4,3,2,1,0:T(8,128)(2,1)S(1)}, bf16[4,2,16,8,1280]{4,3,2,1,0:T(8,128)(2,1)}, u32[]{:S(2)}) %copy-start) | copy-done | bytes 2621464
  6.6 1.3 %copy-done.2 = f32[2,16,8,1280]{3,2,1,0:T(8,128)S(1)} copy-done((f32[2,16,8,1280]{3,2,1,0:T(8,128)S(1)}, f32[2,16,8,1280]{3,2,1,0:T(8,128)}, u32[]{:S(2)}) %copy-start.2) | copy-done | bytes 1310744
  9.8 3.0 %collective-permute-start.2 = (f32[16,4,1280]{2,1,0:T(4,128)S(1)}, f32[16,4,1280]{2,1,0:T(4,128)}, u32[]{:S(2)}, u32[]{:S(2)}) collective-permute-start(f32[16,4,1280]{2,1,0:T(4,128)S(1)} %get-tuple-element.30), channel_id=1, source_target_pairs={{1,2},{2,1},{5,6},{6,5},{9,10},{10,9},{13,14},{14,13},{17,18},{18,... | collective-permute-start | bytes 983048 | tf_op jit(solution)/shard_map/ppermute | solution.py:237
  13.0 2.5 %collective-permute-start.4 = (f32[17,4,1280]{2,1,0:T(4,128)S(1)}, f32[17,4,1280]{2,1,0:T(4,128)S(1)}, u32[]{:S(2)}, u32[]{:S(2)}) collective-permute-start(f32[17,4,1280]{2,1,0:T(4,128)S(1)} %get-tuple-element.32), channel_id=1, source_target_pairs={{1,2},{2,1},{5,6},{6,5},{9,10},{10,9},{13,14},{14,13},{17,18},{18,... | collective-permute-start | bytes 1044488 | tf_op jit(solution)/shard_map/ppermute | solution.py:237
  15.6 2.9 %collective-permute-done.2 = f32[16,4,1280]{2,1,0:T(4,128)} collective-permute-done((f32[16,4,1280]{2,1,0:T(4,128)S(1)}, f32[16,4,1280]{2,1,0:T(4,128)}, u32[]{:S(2)}, u32[]{:S(2)}) %collective-permute-start.2) | collective-permute-done | bytes 327712 | tf_op jit(solution)/shard_map/ppermute | solution.py:237
  19.7 2.2 %collective-permute-done.4 = f32[17,4,1280]{2,1,0:T(4,128)S(1)} collective-permute-done((f32[17,4,1280]{2,1,0:T(4,128)S(1)}, f32[17,4,1280]{2,1,0:T(4,128)S(1)}, u32[]{:S(2)}, u32[]{:S(2)}) %collective-permute-start.4) | collective-permute-done | bytes 348192 | tf_op jit(solution)/shard_map/ppermute | solution.py:237
  22.3 1.4 %copy-done.1 = bf16[4,2,16,8,1280]{4,3,2,1,0:T(8,128)(2,1)S(1)} copy-done((bf16[4,2,16,8,1280]{4,3,2,1,0:T(8,128)(2,1)S(1)}, bf16[4,2,16,8,1280]{4,3,2,1,0:T(8,128)(2,1)}, u32[]{:S(2)}) %copy-start.1) | copy-done | bytes 2621464
  23.7 5.1 %shard_map.80 = (f32[4,2,8,1280]{3,2,1,0:T(8,128)S(1)}, f32[4,2,8,1280]{3,2,1,0:T(8,128)S(1)}, f32[4,2,8,1280]{3,2,1,0:T(8,128)S(1)}, f32[4,2,8,1280]{3,2,1,0:T(8,128)S(1)}) custom-call(f32[2,16,8,1280]{3,2,1,0:T(8,128)S(1)} %copy-done.3, f32[17,8,1280]{2,1,0:T(8,128)S(1)} %pad_maximum_fusion.beyond, f32[8,1280]{1,0:T(8,128)S(1)} %fusion.13.k_beyond, ...), custom_call_target="tpu_custom_call" | custom-call | tf_op jit(solution)/shard_map/pallas_call | solution.py:215
  30.6 5.2 %shard_map.78 = (f32[4,2,8,1280]{3,2,1,0:T(8,128)S(1)}, f32[4,2,8,1280]{3,2,1,0:T(8,128)S(1)}, f32[4,2,8,1280]{3,2,1,0:T(8,128)S(1)}, f32[4,2,8,1280]{3,2,1,0:T(8,128)S(1)}) custom-call(f32[2,16,8,1280]{3,2,1,0:T(8,128)S(1)} %copy-done.3, f32[16,8,1280]{2,1,0:T(8,128)S(1)} %pad_maximum_fusion.1.beyond, f32[8,1280]{1,0:T(8,128)S(1)} %fusion.13.k_beyond, ...), custom_call_target="tpu_custom_call" | custom-call | tf_op jit(solution)/shard_map/pallas_call | solution.py:215
  38.6 1.4 %collective-permute-start.18 = (f32[2,2,8,1280]{3,2,1,0:T(8,128)S(1)}, f32[2,2,8,1280]{3,2,1,0:T(8,128)S(1)}, u32[]{:S(2)}, u32[]{:S(2)}) collective-permute-start(f32[2,2,8,1280]{3,2,1,0:T(8,128)S(1)} %slice_add_fusion.2), channel_id=1, source_target_pairs={{0,8},{4,12},{8,0},{12,4},{16,24},{20,28},{24,16},{28,20},{1,9},{5... | collective-permute-start | bytes 491528 | tf_op jit(solution)/shard_map/ppermute | solution.py:227
  40.0 5.6 %collective-permute-done.22 = f32[4,2,8,1280]{3,2,1,0:T(8,128)S(1)} collective-permute-done((f32[4,2,8,1280]{3,2,1,0:T(8,128)S(1)}, f32[4,2,8,1280]{3,2,1,0:T(8,128)S(1)}, u32[]{:S(2)}, u32[]{:S(2)}) %collective-permute-start.22) | collective-permute-done | bytes 327712 | tf_op jit(solution)/shard_map/ppermute | solution.py:227
  45.7 1.4 %collective-permute-start.23 = (f32[2,2,8,1280]{3,2,1,0:T(8,128)S(1)}, f32[2,2,8,1280]{3,2,1,0:T(8,128)S(1)}, u32[]{:S(2)}, u32[]{:S(2)}) collective-permute-start(f32[2,2,8,1280]{3,2,1,0:T(8,128)S(1)} %slice_add_fusion), channel_id=1, source_target_pairs={{0,8},{4,12},{8,0},{12,4},{16,24},{20,28},{24,16},{28,20},{1,9},{5... | collective-permute-start | bytes 491528 | tf_op jit(solution)/shard_map/ppermute | solution.py:227
  47.0 5.1 %collective-permute-done.5 = f32[4,2,8,1280]{3,2,1,0:T(8,128)S(1)} collective-permute-done((f32[4,2,8,1280]{3,2,1,0:T(8,128)S(1)}, f32[4,2,8,1280]{3,2,1,0:T(8,128)S(1)}, u32[]{:S(2)}, u32[]{:S(2)}) %collective-permute-start.5) | collective-permute-done | bytes 327712 | tf_op jit(solution)/shard_map/ppermute | solution.py:227
  56.6 2.4 %collective-permute-done.6 = f32[2,2,8,1280]{3,2,1,0:T(8,128)S(1)} collective-permute-done((f32[2,2,8,1280]{3,2,1,0:T(8,128)S(1)}, f32[2,2,8,1280]{3,2,1,0:T(8,128)S(1)}, u32[]{:S(2)}, u32[]{:S(2)}) %collective-permute-start.6) | collective-permute-done | bytes 163872 | tf_op jit(solution)/shard_map/ppermute | solution.py:227
  59.3 2.4 %collective-permute-start.12 = (f32[2,2,8,1280]{3,2,1,0:T(8,128)S(1)}, f32[2,2,8,1280]{3,2,1,0:T(8,128)S(1)}, u32[]{:S(2)}, u32[]{:S(2)}) collective-permute-start(f32[2,2,8,1280]{3,2,1,0:T(8,128)S(1)} %pad_maximum_fusion.14), channel_id=1, source_target_pairs={{0,16},{4,20},{8,24},{12,28},{16,0},{20,4},{24,8},{28,12},{1,17},{... | collective-permute-start | bytes 491528 | tf_op jit(solution)/shard_map/ppermute | solution.py:227
  61.7 12.7 %collective-permute-done.19 = f32[2,2,8,1280]{3,2,1,0:T(8,128)S(1)} collective-permute-done((f32[2,2,8,1280]{3,2,1,0:T(8,128)S(1)}, f32[2,2,8,1280]{3,2,1,0:T(8,128)S(1)}, u32[]{:S(2)}, u32[]{:S(2)}) %collective-permute-start.19) | collective-permute-done | bytes 163872 | tf_op jit(solution)/shard_map/ppermute | solution.py:227
  74.5 3.4 %collective-permute-done.24 = f32[2,2,8,1280]{3,2,1,0:T(8,128)S(1)} collective-permute-done((f32[2,2,8,1280]{3,2,1,0:T(8,128)S(1)}, f32[2,2,8,1280]{3,2,1,0:T(8,128)S(1)}, u32[]{:S(2)}, u32[]{:S(2)}) %collective-permute-start.24) | collective-permute-done | bytes 163872 | tf_op jit(solution)/shard_map/ppermute | solution.py:227
  78.0 3.4 %collective-permute-done.7 = f32[2,2,8,1280]{3,2,1,0:T(8,128)S(1)} collective-permute-done((f32[2,2,8,1280]{3,2,1,0:T(8,128)S(1)}, f32[2,2,8,1280]{3,2,1,0:T(8,128)S(1)}, u32[]{:S(2)}, u32[]{:S(2)}) %collective-permute-start.7) | collective-permute-done | bytes 163872 | tf_op jit(solution)/shard_map/ppermute | solution.py:227
  81.6 3.4 %collective-permute-done.12 = f32[2,2,8,1280]{3,2,1,0:T(8,128)S(1)} collective-permute-done((f32[2,2,8,1280]{3,2,1,0:T(8,128)S(1)}, f32[2,2,8,1280]{3,2,1,0:T(8,128)S(1)}, u32[]{:S(2)}, u32[]{:S(2)}) %collective-permute-start.12) | collective-permute-done | bytes 163872 | tf_op jit(solution)/shard_map/ppermute | solution.py:227
  85.4 3.8 %collective-permute-done.20 = f32[2,2,8,1280]{3,2,1,0:T(8,128)S(1)} collective-permute-done((f32[2,2,8,1280]{3,2,1,0:T(8,128)S(1)}, f32[2,2,8,1280]{3,2,1,0:T(8,128)S(1)}, u32[]{:S(2)}, u32[]{:S(2)}) %collective-permute-start.20) | collective-permute-done | bytes 163872 | tf_op jit(solution)/shard_map/ppermute | solution.py:227
  89.6 3.2 %collective-permute-done.25 = f32[2,2,8,1280]{3,2,1,0:T(8,128)S(1)} collective-permute-done((f32[2,2,8,1280]{3,2,1,0:T(8,128)S(1)}, f32[2,2,8,1280]{3,2,1,0:T(8,128)S(1)}, u32[]{:S(2)}, u32[]{:S(2)}) %collective-permute-start.25) | collective-permute-done | bytes 163872 | tf_op jit(solution)/shard_map/ppermute | solution.py:227
  93.1 3.2 %collective-permute-done.8 = f32[2,2,8,1280]{3,2,1,0:T(8,128)S(1)} collective-permute-done((f32[2,2,8,1280]{3,2,1,0:T(8,128)S(1)}, f32[2,2,8,1280]{3,2,1,0:T(8,128)S(1)}, u32[]{:S(2)}, u32[]{:S(2)}) %collective-permute-start.8) | collective-permute-done | bytes 163872 | tf_op jit(solution)/shard_map/ppermute | solution.py:227
  96.7 1.3 %collective-permute-done.21.refs_1_ = f32[4,2,8,1280]{3,2,1,0:T(8,128)S(1)} collective-permute-done((f32[4,2,8,1280]{3,2,1,0:T(8,128)S(1)}, f32[4,2,8,1280]{3,2,1,0:T(8,128)S(1)}, u32[]{:S(2)}, u32[]{:S(2)}) %collective-permute-start.21) | collective-permute-done | bytes 327712 | tf_op jit(solution)/shard_map/ppermute | solution.py:227
  98.0 7.0 %collective-permute-done.26.refs_3_ = f32[4,2,8,1280]{3,2,1,0:T(8,128)S(1)} collective-permute-done((f32[4,2,8,1280]{3,2,1,0:T(8,128)S(1)}, f32[4,2,8,1280]{3,2,1,0:T(8,128)S(1)}, u32[]{:S(2)}, u32[]{:S(2)}) %collective-permute-start.26) | collective-permute-done | bytes 327712 | tf_op jit(solution)/shard_map/ppermute | solution.py:227
  105.4 2.5 %collective-permute-start.27 = (f32[16,4,1280]{2,1,0:T(4,128)S(1)}, f32[16,4,1280]{2,1,0:T(4,128)S(1)}, u32[]{:S(2)}, u32[]{:S(2)}) collective-permute-start(f32[16,4,1280]{2,1,0:T(4,128)S(1)} %get-tuple-element.52), channel_id=1, source_target_pairs={{0,1},{1,0},{2,3},{3,2},{4,5},{5,4},{6,7},{7,6},{8,9},{9,8},{10,11... | collective-permute-start | bytes 983048 | tf_op jit(solution)/shard_map/ppermute | solution.py:232
  108.0 1.9 %collective-permute-start.28 = (f32[16,4,1280]{2,1,0:T(4,128)S(1)}, f32[16,4,1280]{2,1,0:T(4,128)S(1)}, u32[]{:S(2)}, u32[]{:S(2)}) collective-permute-start(f32[16,4,1280]{2,1,0:T(4,128)S(1)} %get-tuple-element.53), channel_id=1, source_target_pairs={{1,2},{2,1},{5,6},{6,5},{9,10},{10,9},{13,14},{14,13},{17,18},{18,... | collective-permute-start | bytes 983048 | tf_op jit(solution)/shard_map/ppermute | solution.py:237
  110.7 1.3 %collective-permute-done.9.refs_1_ = f32[4,2,8,1280]{3,2,1,0:T(8,128)S(1)} collective-permute-done((f32[4,2,8,1280]{3,2,1,0:T(8,128)S(1)}, f32[4,2,8,1280]{3,2,1,0:T(8,128)S(1)}, u32[]{:S(2)}, u32[]{:S(2)}) %collective-permute-start.9) | collective-permute-done | bytes 327712 | tf_op jit(solution)/shard_map/ppermute | solution.py:227
  112.5 1.5 %collective-permute-start.15 = (f32[16,4,1280]{2,1,0:T(4,128)S(1)}, f32[16,4,1280]{2,1,0:T(4,128)S(1)}, u32[]{:S(2)}, u32[]{:S(2)}) collective-permute-start(f32[16,4,1280]{2,1,0:T(4,128)S(1)} %get-tuple-element.41), channel_id=1, source_target_pairs={{0,1},{1,0},{2,3},{3,2},{4,5},{5,4},{6,7},{7,6},{8,9},{9,8},{10,11... | collective-permute-start | bytes 983048 | tf_op jit(solution)/shard_map/ppermute | solution.py:232
  114.0 1.9 %collective-permute-start.16 = (f32[16,4,1280]{2,1,0:T(4,128)S(1)}, f32[16,4,1280]{2,1,0:T(4,128)S(1)}, u32[]{:S(2)}, u32[]{:S(2)}) collective-permute-start(f32[16,4,1280]{2,1,0:T(4,128)S(1)} %get-tuple-element.42), channel_id=1, source_target_pairs={{1,2},{2,1},{5,6},{6,5},{9,10},{10,9},{13,14},{14,13},{17,18},{18,... | collective-permute-start | bytes 983048 | tf_op jit(solution)/shard_map/ppermute | solution.py:237
  116.6 5.7 %shard_map.82.refs_0_ = f32[2,16,8,1280]{3,2,1,0:T(8,128)} custom-call(f32[2,16,8,1280]{3,2,1,0:T(8,128)S(1)} %copy-done.3, f32[2,8,8,1280]{3,2,1,0:T(8,128)S(1)} %get-tuple-element.51.back, f32[16,8,1280]{2,1,0:T(8,128)S(1)} %pad_maximum_fusion.3.beyond, f32[8,1280]{1,0:T(8,128)S(1)} %fusion.13.k_beyond, f32[8,1280]{1,0:T(8,128)S(1)} %copy-done.5), custom_call_target="tpu_custom_call" | custom-call | tf_op jit(solution)/shard_map/pallas_call | solution.py:320
  122.6 5.8 %shard_map.83 = f32[2,16,8,1280]{3,2,1,0:T(8,128)} custom-call(f32[2,16,8,1280]{3,2,1,0:T(8,128)S(1)} %copy-done.3, f32[2,8,8,1280]{3,2,1,0:T(8,128)S(1)} %get-tuple-element.40.back, f32[16,8,1280]{2,1,0:T(8,128)S(1)} %pad_maximum_fusion.2.beyond, f32[8,1280]{1,0:T(8,128)S(1)} %fusion.13.k_beyond, ...), custom_call_target="tpu_custom_call", output_to_operand_aliasing={{}: (5, {})} | custom-call | tf_op jit(solution)/shard_map/pallas_call | solution.py:320
  (102 shorter events, 18.3 us)
Async XLA Ops:
  1.6 18.0 %collective-permute-start = (f32[4,2,8,1280]{3,2,0,1:T(8,128)S(1)}, f32[4,2,8,1280]{3,2,0,1:T(8,128)S(1)}, u32[]{:S(2)}, u32[]{:S(2)}) collective-permute-start(f32[4,2,8,1280]{3,2,0,1:T(8,128)S(1)} %copy.10), channel_id=1, source_target_pairs={{0,16},{4,20},{8,24},{12,28},{16,0},{20,4},{24,8},{28,12},{1,17},{... | collective-permute-start | bytes 983048 | tf_op jit(solution)/shard_map/ppermute | solution.py:227
  8.7 6.8 %copy-start.7 = (f32[4,2,8,1280]{3,2,1,0:T(8,128)S(1)}, f32[4,2,8,1280]{3,2,1,0:T(8,128)}, u32[]{:S(2)}) copy-start(f32[4,2,8,1280]{3,2,1,0:T(8,128)} %param.10) | copy-start | bytes 983044
  8.7 6.9 %copy-start.8 = (f32[4,2,8,1280]{3,2,1,0:T(8,128)S(1)}, f32[4,2,8,1280]{3,2,1,0:T(8,128)}, u32[]{:S(2)}) copy-start(f32[4,2,8,1280]{3,2,1,0:T(8,128)} %param.11) | copy-start | bytes 983044
  8.8 6.8 %collective-permute-start.1 = (f32[16,4,1280]{2,1,0:T(4,128)S(1)}, f32[16,4,1280]{2,1,0:T(4,128)}, u32[]{:S(2)}, u32[]{:S(2)}) collective-permute-start(f32[16,4,1280]{2,1,0:T(4,128)S(1)} %get-tuple-element.29), channel_id=1, source_target_pairs={{0,1},{1,0},{2,3},{3,2},{4,5},{5,4},{6,7},{7,6},{8,9},{9,8},{10,11... | collective-permute-start | bytes 983048 | tf_op jit(solution)/shard_map/ppermute | solution.py:232
  9.8 8.7 %collective-permute-start.2 = (f32[16,4,1280]{2,1,0:T(4,128)S(1)}, f32[16,4,1280]{2,1,0:T(4,128)}, u32[]{:S(2)}, u32[]{:S(2)}) collective-permute-start(f32[16,4,1280]{2,1,0:T(4,128)S(1)} %get-tuple-element.30), channel_id=1, source_target_pairs={{1,2},{2,1},{5,6},{6,5},{9,10},{10,9},{13,14},{14,13},{17,18},{18,... | collective-permute-start | bytes 983048 | tf_op jit(solution)/shard_map/ppermute | solution.py:237
  12.9 6.8 %collective-permute-start.3 = (f32[17,4,1280]{2,1,0:T(4,128)S(1)}, f32[17,4,1280]{2,1,0:T(4,128)S(1)}, u32[]{:S(2)}, u32[]{:S(2)}) collective-permute-start(f32[17,4,1280]{2,1,0:T(4,128)S(1)} %get-tuple-element.31), channel_id=1, source_target_pairs={{0,1},{1,0},{2,3},{3,2},{4,5},{5,4},{6,7},{7,6},{8,9},{9,8},{10,11... | collective-permute-start | bytes 1044488 | tf_op jit(solution)/shard_map/ppermute | solution.py:232
  13.0 9.0 %collective-permute-start.4 = (f32[17,4,1280]{2,1,0:T(4,128)S(1)}, f32[17,4,1280]{2,1,0:T(4,128)S(1)}, u32[]{:S(2)}, u32[]{:S(2)}) collective-permute-start(f32[17,4,1280]{2,1,0:T(4,128)S(1)} %get-tuple-element.32), channel_id=1, source_target_pairs={{1,2},{2,1},{5,6},{6,5},{9,10},{10,9},{13,14},{14,13},{17,18},{18,... | collective-permute-start | bytes 1044488 | tf_op jit(solution)/shard_map/ppermute | solution.py:237
  19.7 2.6 %copy-start.3 = (f32[2,16,8,1280]{3,2,1,0:T(8,128)S(1)}, f32[2,16,8,1280]{3,2,1,0:T(8,128)}, u32[]{:S(2)}) copy-start(f32[2,16,8,1280]{3,2,1,0:T(8,128)} %alpha.9) | copy-start | bytes 3932164
  28.8 9.8 %collective-permute-start.17 = (f32[4,2,8,1280]{3,2,1,0:T(8,128)S(1)}, f32[4,2,8,1280]{3,2,1,0:T(8,128)S(1)}, u32[]{:S(2)}, u32[]{:S(2)}) collective-permute-start(f32[4,2,8,1280]{3,2,1,0:T(8,128)S(1)} %get-tuple-element.45), channel_id=1, source_target_pairs={{0,4},{4,0},{8,12},{12,8},{16,20},{20,16},{24,28},{28,24},{1,5},{5... | collective-permute-start | bytes 983048 | tf_op jit(solution)/shard_map/ppermute | solution.py:227
  30.3 15.4 %collective-permute-start.22 = (f32[4,2,8,1280]{3,2,1,0:T(8,128)S(1)}, f32[4,2,8,1280]{3,2,1,0:T(8,128)S(1)}, u32[]{:S(2)}, u32[]{:S(2)}) collective-permute-start(f32[4,2,8,1280]{3,2,1,0:T(8,128)S(1)} %get-tuple-element.49), channel_id=1, source_target_pairs={{0,4},{4,0},{8,12},{12,8},{16,20},{20,16},{24,28},{28,24},{1,5},{5... | collective-permute-start | bytes 983048 | tf_op jit(solution)/shard_map/ppermute | solution.py:227
  35.8 16.3 %collective-permute-start.5 = (f32[4,2,8,1280]{3,2,1,0:T(8,128)S(1)}, f32[4,2,8,1280]{3,2,1,0:T(8,128)S(1)}, u32[]{:S(2)}, u32[]{:S(2)}) collective-permute-start(f32[4,2,8,1280]{3,2,1,0:T(8,128)S(1)} %get-tuple-element.34), channel_id=1, source_target_pairs={{0,4},{4,0},{8,12},{12,8},{16,20},{20,16},{24,28},{28,24},{1,5},{5... | collective-permute-start | bytes 983048 | tf_op jit(solution)/shard_map/ppermute | solution.py:227
  37.1 15.6 %collective-permute-start.10 = (f32[4,2,8,1280]{3,2,1,0:T(8,128)S(1)}, f32[4,2,8,1280]{3,2,1,0:T(8,128)S(1)}, u32[]{:S(2)}, u32[]{:S(2)}) collective-permute-start(f32[4,2,8,1280]{3,2,1,0:T(8,128)S(1)} %get-tuple-element.38), channel_id=1, source_target_pairs={{0,8},{4,12},{8,0},{12,4},{16,24},{20,28},{24,16},{28,20},{1,9},{5... | collective-permute-start | bytes 983048 | tf_op jit(solution)/shard_map/ppermute | solution.py:227
  38.6 15.3 %collective-permute-start.18 = (f32[2,2,8,1280]{3,2,1,0:T(8,128)S(1)}, f32[2,2,8,1280]{3,2,1,0:T(8,128)S(1)}, u32[]{:S(2)}, u32[]{:S(2)}) collective-permute-start(f32[2,2,8,1280]{3,2,1,0:T(8,128)S(1)} %slice_add_fusion.2), channel_id=1, source_target_pairs={{0,8},{4,12},{8,0},{12,4},{16,24},{20,28},{24,16},{28,20},{1,9},{5... | collective-permute-start | bytes 491528 | tf_op jit(solution)/shard_map/ppermute | solution.py:227
  45.7 9.6 %collective-permute-start.23 = (f32[2,2,8,1280]{3,2,1,0:T(8,128)S(1)}, f32[2,2,8,1280]{3,2,1,0:T(8,128)S(1)}, u32[]{:S(2)}, u32[]{:S(2)}) collective-permute-start(f32[2,2,8,1280]{3,2,1,0:T(8,128)S(1)} %slice_add_fusion), channel_id=1, source_target_pairs={{0,8},{4,12},{8,0},{12,4},{16,24},{20,28},{24,16},{28,20},{1,9},{5... | collective-permute-start | bytes 491528 | tf_op jit(solution)/shard_map/ppermute | solution.py:227
  52.1 6.9 %collective-permute-start.6 = (f32[2,2,8,1280]{3,2,1,0:T(8,128)S(1)}, f32[2,2,8,1280]{3,2,1,0:T(8,128)S(1)}, u32[]{:S(2)}, u32[]{:S(2)}) collective-permute-start(f32[2,2,8,1280]{3,2,1,0:T(8,128)S(1)} %slice_add_fusion.6), channel_id=1, source_target_pairs={{0,8},{4,12},{8,0},{12,4},{16,24},{20,28},{24,16},{28,20},{1,9},{5... | collective-permute-start | bytes 491528 | tf_op jit(solution)/shard_map/ppermute | solution.py:227
  52.7 6.5 %collective-permute-start.11 = (f32[2,2,8,1280]{3,2,1,0:T(8,128)S(1)}, f32[2,2,8,1280]{3,2,1,0:T(8,128)S(1)}, u32[]{:S(2)}, u32[]{:S(2)}) collective-permute-start(f32[2,2,8,1280]{3,2,1,0:T(8,128)S(1)} %slice_add_fusion.4), channel_id=1, source_target_pairs={{0,4},{4,0},{8,12},{12,8},{16,20},{20,16},{24,28},{28,24},{1,5},{5... | collective-permute-start | bytes 491528 | tf_op jit(solution)/shard_map/ppermute | solution.py:227
  54.1 20.3 %collective-permute-start.19 = (f32[2,2,8,1280]{3,2,1,0:T(8,128)S(1)}, f32[2,2,8,1280]{3,2,1,0:T(8,128)S(1)}, u32[]{:S(2)}, u32[]{:S(2)}) collective-permute-start(f32[2,2,8,1280]{3,2,1,0:T(8,128)S(1)} %pad_maximum_fusion.15), channel_id=1, source_target_pairs={{0,16},{4,20},{8,24},{12,28},{16,0},{20,4},{24,8},{28,12},{1,17},{... | collective-permute-start | bytes 491528 | tf_op jit(solution)/shard_map/ppermute | solution.py:227
  55.4 22.5 %collective-permute-start.24 = (f32[2,2,8,1280]{3,2,1,0:T(8,128)S(1)}, f32[2,2,8,1280]{3,2,1,0:T(8,128)S(1)}, u32[]{:S(2)}, u32[]{:S(2)}) collective-permute-start(f32[2,2,8,1280]{3,2,1,0:T(8,128)S(1)} %pad_maximum_fusion.16), channel_id=1, source_target_pairs={{0,16},{4,20},{8,24},{12,28},{16,0},{20,4},{24,8},{28,12},{1,17},{... | collective-permute-start | bytes 491528 | tf_op jit(solution)/shard_map/ppermute | solution.py:227
  59.1 22.3 %collective-permute-start.7 = (f32[2,2,8,1280]{3,2,1,0:T(8,128)S(1)}, f32[2,2,8,1280]{3,2,1,0:T(8,128)S(1)}, u32[]{:S(2)}, u32[]{:S(2)}) collective-permute-start(f32[2,2,8,1280]{3,2,1,0:T(8,128)S(1)} %pad_maximum_fusion.13), channel_id=1, source_target_pairs={{0,16},{4,20},{8,24},{12,28},{16,0},{20,4},{24,8},{28,12},{1,17},{... | collective-permute-start | bytes 491528 | tf_op jit(solution)/shard_map/ppermute | solution.py:227
  59.3 25.7 %collective-permute-start.12 = (f32[2,2,8,1280]{3,2,1,0:T(8,128)S(1)}, f32[2,2,8,1280]{3,2,1,0:T(8,128)S(1)}, u32[]{:S(2)}, u32[]{:S(2)}) collective-permute-start(f32[2,2,8,1280]{3,2,1,0:T(8,128)S(1)} %pad_maximum_fusion.14), channel_id=1, source_target_pairs={{0,16},{4,20},{8,24},{12,28},{16,0},{20,4},{24,8},{28,12},{1,17},{... | collective-permute-start | bytes 491528 | tf_op jit(solution)/shard_map/ppermute | solution.py:227
  74.4 14.8 %collective-permute-start.20 = (f32[2,2,8,1280]{3,2,1,0:T(8,128)S(1)}, f32[2,2,8,1280]{3,2,1,0:T(8,128)S(1)}, u32[]{:S(2)}, u32[]{:S(2)}) collective-permute-start(f32[2,2,8,1280]{3,2,1,0:T(8,128)S(1)} %add_multiply_fusion.1), channel_id=1, source_target_pairs={{0,8},{4,12},{8,0},{12,4},{16,24},{20,28},{24,16},{28,20},{1,9},{5... | collective-permute-start | bytes 491528 | tf_op jit(solution)/shard_map/ppermute | solution.py:227
  77.9 14.8 %collective-permute-start.25 = (f32[2,2,8,1280]{3,2,1,0:T(8,128)S(1)}, f32[2,2,8,1280]{3,2,1,0:T(8,128)S(1)}, u32[]{:S(2)}, u32[]{:S(2)}) collective-permute-start(f32[2,2,8,1280]{3,2,1,0:T(8,128)S(1)} %add_multiply_fusion), channel_id=1, source_target_pairs={{0,8},{4,12},{8,0},{12,4},{16,24},{20,28},{24,16},{28,20},{1,9},{5... | collective-permute-start | bytes 491528 | tf_op jit(solution)/shard_map/ppermute | solution.py:227
  81.5 14.7 %collective-permute-start.8 = (f32[2,2,8,1280]{3,2,1,0:T(8,128)S(1)}, f32[2,2,8,1280]{3,2,1,0:T(8,128)S(1)}, u32[]{:S(2)}, u32[]{:S(2)}) collective-permute-start(f32[2,2,8,1280]{3,2,1,0:T(8,128)S(1)} %add_multiply_fusion.3), channel_id=1, source_target_pairs={{0,8},{4,12},{8,0},{12,4},{16,24},{20,28},{24,16},{28,20},{1,9},{5... | collective-permute-start | bytes 491528 | tf_op jit(solution)/shard_map/ppermute | solution.py:227
  85.0 11.6 %collective-permute-start.13 = (f32[2,2,8,1280]{3,2,1,0:T(8,128)S(1)}, f32[2,2,8,1280]{3,2,1,0:T(8,128)S(1)}, u32[]{:S(2)}, u32[]{:S(2)}) collective-permute-start(f32[2,2,8,1280]{3,2,1,0:T(8,128)S(1)} %add_multiply_fusion.2), channel_id=1, source_target_pairs={{0,4},{4,0},{8,12},{12,8},{16,20},{20,16},{24,28},{28,24},{1,5},{5... | collective-permute-start | bytes 491528 | tf_op jit(solution)/shard_map/ppermute | solution.py:227
  89.3 8.7 %collective-permute-start.21 = (f32[4,2,8,1280]{3,2,1,0:T(8,128)S(1)}, f32[4,2,8,1280]{3,2,1,0:T(8,128)S(1)}, u32[]{:S(2)}, u32[]{:S(2)}) collective-permute-start(f32[4,2,8,1280]{3,2,1,0:T(8,128)S(1)} %pad_maximum_fusion.6.refs_0_), channel_id=1, source_target_pairs={{0,4},{4,0},{8,12},{12,8},{16,20},{20,16},{24,28},{28,24},{1,5},{5... | collective-permute-start | bytes 983048 | tf_op jit(solution)/shard_map/ppermute | solution.py:227
  92.8 12.3 %collective-permute-start.26 = (f32[4,2,8,1280]{3,2,1,0:T(8,128)S(1)}, f32[4,2,8,1280]{3,2,1,0:T(8,128)S(1)}, u32[]{:S(2)}, u32[]{:S(2)}) collective-permute-start(f32[4,2,8,1280]{3,2,1,0:T(8,128)S(1)} %pad_maximum_fusion.7.refs_2_), channel_id=1, source_target_pairs={{0,4},{4,0},{8,12},{12,8},{16,20},{20,16},{24,28},{28,24},{1,5},{5... | collective-permute-start | bytes 983048 | tf_op jit(solution)/shard_map/ppermute | solution.py:227
  96.3 15.8 %collective-permute-start.9 = (f32[4,2,8,1280]{3,2,1,0:T(8,128)S(1)}, f32[4,2,8,1280]{3,2,1,0:T(8,128)S(1)}, u32[]{:S(2)}, u32[]{:S(2)}) collective-permute-start(f32[4,2,8,1280]{3,2,1,0:T(8,128)S(1)} %pad_maximum_fusion.4.refs_0_), channel_id=1, source_target_pairs={{0,4},{4,0},{8,12},{12,8},{16,20},{20,16},{24,28},{28,24},{1,5},{5... | collective-permute-start | bytes 983048 | tf_op jit(solution)/shard_map/ppermute | solution.py:227
  96.6 15.4 %collective-permute-start.14 = (f32[4,2,8,1280]{3,2,1,0:T(8,128)S(1)}, f32[4,2,8,1280]{3,2,1,0:T(8,128)S(1)}, u32[]{:S(2)}, u32[]{:S(2)}) collective-permute-start(f32[4,2,8,1280]{3,2,1,0:T(8,128)S(1)} %pad_maximum_fusion.5.refs_2_), channel_id=1, source_target_pairs={{0,8},{4,12},{8,0},{12,4},{16,24},{20,28},{24,16},{28,20},{1,9},{5... | collective-permute-start | bytes 983048 | tf_op jit(solution)/shard_map/ppermute | solution.py:227
  105.4 10.5 %collective-permute-start.27 = (f32[16,4,1280]{2,1,0:T(4,128)S(1)}, f32[16,4,1280]{2,1,0:T(4,128)S(1)}, u32[]{:S(2)}, u32[]{:S(2)}) collective-permute-start(f32[16,4,1280]{2,1,0:T(4,128)S(1)} %get-tuple-element.52), channel_id=1, source_target_pairs={{0,1},{1,0},{2,3},{3,2},{4,5},{5,4},{6,7},{7,6},{8,9},{9,8},{10,11... | collective-permute-start | bytes 983048 | tf_op jit(solution)/shard_map/ppermute | solution.py:232
  108.0 8.4 %collective-permute-start.28 = (f32[16,4,1280]{2,1,0:T(4,128)S(1)}, f32[16,4,1280]{2,1,0:T(4,128)S(1)}, u32[]{:S(2)}, u32[]{:S(2)}) collective-permute-start(f32[16,4,1280]{2,1,0:T(4,128)S(1)} %get-tuple-element.53), channel_id=1, source_target_pairs={{1,2},{2,1},{5,6},{6,5},{9,10},{10,9},{13,14},{14,13},{17,18},{18,... | collective-permute-start | bytes 983048 | tf_op jit(solution)/shard_map/ppermute | solution.py:237
  112.5 9.8 %collective-permute-start.15 = (f32[16,4,1280]{2,1,0:T(4,128)S(1)}, f32[16,4,1280]{2,1,0:T(4,128)S(1)}, u32[]{:S(2)}, u32[]{:S(2)}) collective-permute-start(f32[16,4,1280]{2,1,0:T(4,128)S(1)} %get-tuple-element.41), channel_id=1, source_target_pairs={{0,1},{1,0},{2,3},{3,2},{4,5},{5,4},{6,7},{7,6},{8,9},{9,8},{10,11... | collective-permute-start | bytes 983048 | tf_op jit(solution)/shard_map/ppermute | solution.py:232
  114.0 8.4 %collective-permute-start.16 = (f32[16,4,1280]{2,1,0:T(4,128)S(1)}, f32[16,4,1280]{2,1,0:T(4,128)S(1)}, u32[]{:S(2)}, u32[]{:S(2)}) collective-permute-start(f32[16,4,1280]{2,1,0:T(4,128)S(1)} %get-tuple-element.42), channel_id=1, source_target_pairs={{1,2},{2,1},{5,6},{6,5},{9,10},{10,9},{13,14},{14,13},{17,18},{18,... | collective-permute-start | bytes 983048 | tf_op jit(solution)/shard_map/ppermute | solution.py:237
  (6 other events, 8.7 us)

commit v2 on v1

--- a/solution.py
+++ b/solution.py
@@ -80,52 +80,100 @@
     return index
 
 
-def edges_kernel(width, alpha, kappa, perturb, *outs):
+def edges_kernel(width, alpha, kappa, *refs):
+    held, cells, done = refs[-3:]
+    outs = refs[:-3]
     members = alpha.shape[0]
     count = alpha.shape[1] // width
     even = lax.rem(lax.axis_index("space"), 2) == 0
 
+    def copy(m):
+        return pltpu.make_async_copy(alpha.at[m], held.at[m], done.at[m])
+
     def send(chunk, at, rows):
         outs[2 * chunk][at] = jnp.where(even, rows[4:], rows[:4])
         outs[2 * chunk + 1][at] = jnp.where(even, rows[:4], rows[4:])
 
-    def level(piece, carry):
-        for chunk in range(width):
-            for m in range(members):
-                send(chunk, m * count + piece, alpha[m, piece * width + chunk])
-        return carry
-
-    lax.fori_loop(0, count, level, 0)
-    send(0, members * count, kappa[...])
-
-
-def forward_kernel(chunk, width, groups, alpha, beyond, k_beyond, kappa, land, perturb, *refs):
+    last = pltpu.make_async_copy(kappa, cells, done.at[members])
+    for m in range(members):
+        copy(m).start()
+    last.start()
+    for m in range(members):
+        copy(m).wait()
+
+        def level(piece, carry, m=m):
+            for chunk in range(width):
+                send(chunk, m * count + piece, held[m, piece * width + chunk])
+            return carry
+
+        lax.fori_loop(0, count, level, 0)
+    last.wait()
+    send(0, members * count, cells[...])
+
+
+def forward_kernel(chunk, width, groups, parts, fetches, alpha, perturb, beyond, k_beyond, kappa, land, *refs):
+    if fetches:
+        fields, scales, got_field, got_scale = refs[-4:]
+        refs = refs[:-4]
     faces, pair, outs = refs[-2], refs[-1], refs[:-2]
-    members = perturb.shape[1]
-    count = 2 * outs[0].shape[0]
+    _, members = perturb.shape[:2]
+    count = alpha.shape[1] // width
     me = lax.axis_index("member")
+    lead = groups[0][1]
+
+    def owner_of(part, i):
+        return place_of(i, lead[1:]) + parts[part] * lead[0]
+
+    def copies(part, i):
+        row = (owner_of(part, i) ^ me) * width + chunk
+        at = part * (count // 2) + i
+        return (
+            pltpu.make_async_copy(alpha.at[:, row], fields.at[at], got_field.at[at]),
+            pltpu.make_async_copy(perturb.at[:, :, row], scales.at[at], got_scale.at[at]),
+        )
+
+    for part in range(len(parts) if fetches else 0):
+        def fetch(i, carry, part=part):
+            for copy in copies(part, i):
+                copy.start()
+            return carry
+
+        lax.fori_loop(0, count // 2, fetch, 0)
     fill_faces(faces, pair.at[0], kappa[...], k_beyond[...])
-    lead = groups[0][1]
-    for half in (1, 0):
-        def level(i, carry, half=half):
-            owner = place_of(i, lead[1:]) + half * lead[0]
+    for part, half in enumerate(parts):
+        def level(i, carry, part=part, half=half):
+            owner = owner_of(part, i)
             piece = owner ^ me
             row = piece * width + chunk
+            if fetches:
+                for copy in copies(part, i):
+                    copy.wait()
+                here = part * (count // 2) + i
+                field = [fields[here, m] for m in range(members)]
+                scale = lambda t, m: scales[here, t, m].astype(F32)
+            else:
+                field = [alpha[m, row] for m in range(members)]
+                scale = lambda t, m: perturb[t, m, row].astype(F32)
             local = []
             for m in range(members):
-                local.append(diffuse(faces, pair.at[m], alpha[m, row], beyond[m * count + piece]) * land[...].astype(F32))
+                value = diffuse(faces, pair.at[m], field[m], beyond[m * count + piece])
+                local.append(value * land[...].astype(F32))
 
             def added(t):
-                total = perturb[t, 0, row].astype(F32) * local[0]
+                total = scale(t, 0) * local[0]
                 for m in range(1, members):
-                    total = total + perturb[t, m, row].astype(F32) * local[m]
+                    total = total + scale(t, m) * local[m]
                 return total
 
             for g, (slots, order) in enumerate(groups):
-                send, keep = outs[2 * g : 2 * g + 2]
+                if len(parts) == 1:
+                    out = outs[g]
+                else:
+                    send, keep = outs[2 * g : 2 * g + 2]
+                    out = send if half else keep
                 if order == lead:
                     for k, t in enumerate(slots):
-                        (send if half else keep)[i, k] = added(t)
+                        out[i, k] = added(t)
                 else:
                     at = index_of(owner, order[1:])
                     sends = (owner & order[0]) != 0
@@ -181,20 +229,21 @@
         lax.fori_loop(0, count // 2, level, 0)
 
 
-def adjoint_kernel(chunk, width, alpha, back, beyond, k_beyond, kappa, *refs):
+def adjoint_kernel(chunk, width, span, alpha, back, beyond, k_beyond, kappa, *refs):
     gradient, faces, pair, stage, done = refs[-5:]
     members, count = back.shape[:2]
     fill_faces(faces, pair.at[0], kappa[...], k_beyond[...])
 
     def copy(m, piece):
+        at = piece - span[0]
         return pltpu.make_async_copy(
-            stage.at[m, piece], gradient.at[m, piece * width + chunk], done.at[m, piece]
+            stage.at[m, at], gradient.at[m, piece * width + chunk], done.at[m, at]
         )
 
     def level(piece, carry):
         for m in range(members):
             value = diffuse(faces, pair.at[m], back[m, piece], beyond[m * count + piece])
-            stage[m, piece] = value + alpha[m, piece * width + chunk]
+            stage[m, piece - span[0]] = value + alpha[m, piece * width + chunk]
             copy(m, piece).start()
         return carry
 
@@ -203,21 +252,25 @@
             copy(m, piece).wait()
         return carry
 
-    lax.fori_loop(0, count, level, 0)
-    lax.fori_loop(0, count, finish, 0)
+    lax.fori_loop(*span, level, 0)
+    lax.fori_loop(*span, finish, 0)
 
 
 VMEM = pl.BlockSpec(memory_space=pltpu.VMEM)
-GRANT = pltpu.CompilerParams(vmem_limit_bytes=24 << 20)
-
-
-def call(kernel, args, outs, scratch=()):
+GRANT = pltpu.CompilerParams(vmem_limit_bytes=8 << 20)
+
+
+HERE = pl.BlockSpec(memory_space=pltpu.HBM)
+
+
+def call(kernel, args, outs, scratch=(), left=0):
+    args = [pltpu.with_memory_space_constraint(x, pltpu.HBM) if k < left else x for k, x in enumerate(args)]
     return pl.pallas_call(
         kernel,
         out_shape=[jax.ShapeDtypeStruct(shape, F32) for shape in outs],
-        in_specs=[VMEM] * len(args),
+        in_specs=[HERE] * left + [VMEM] * (len(args) - left),
         out_specs=[VMEM] * len(outs),
-        scratch_shapes=[pltpu.VMEM(shape, F32) for shape in scratch],
+        scratch_shapes=list(scratch),
         compiler_params=GRANT,
     )(*args)
 
@@ -272,7 +325,17 @@
     plans.append(((early, bits), (late, swapped)))
 
     shapes = [(members * count + (c == 0), 4, lon) for c in range(width) for _ in range(2)]
-    edges = call(functools.partial(edges_kernel, width), (alpha, kappa, perturb), shapes)
+    edges = call(
+        functools.partial(edges_kernel, width),
+        (alpha, kappa),
+        shapes,
+        [
+            pltpu.VMEM(alpha.shape, F32),
+            pltpu.VMEM(kappa.shape, F32),
+            pltpu.SemaphoreType.DMA((members + 1,)),
+        ],
+        left=2,
+    )
     beyond = [halves(edges[2 * c], edges[2 * c + 1]) for c in range(width)]
     k_beyond = beyond[0][-1]
 
@@ -287,17 +350,36 @@
     misfits = [[] for _ in range(width)]
     parts = [[] for _ in range(width)]
     for c in range(width):
-        half = (count // 2,)
-        shapes = [half + (len(group), rows, lon) for group, order in plans[c] for _ in range(2)]
-        sums = call(
-            functools.partial(forward_kernel, c, width, plans[c]),
-            (alpha, beyond[c], k_beyond, kappa, land, perturb),
-            shapes,
-            [(10, rows, lon), (members, lon // LANES, 2 * rows, LANES)],
-        )
+        half = count // 2
+        whole = any(order != bits for group, order in plans[c])
+        sums = [[], []]
+        for name, parts_of in (("", (1, 0)),) if whole else (("a", (1,)), ("b", (0,))):
+            room = half * len(parts_of)
+            scratch = [
+                pltpu.VMEM((10, rows, lon), F32),
+                pltpu.VMEM((members, lon // LANES, 2 * rows, LANES), F32),
+            ]
+            fetches = name == "a"
+            if fetches:
+                scratch += [
+                    pltpu.VMEM((room, members, rows, lon), F32),
+                    pltpu.VMEM((room, slots, members, rows, lon), perturb.dtype),
+                    pltpu.SemaphoreType.DMA((room,)),
+                    pltpu.SemaphoreType.DMA((room,)),
+                ]
+            made = call(
+                functools.partial(forward_kernel, c, width, plans[c], parts_of, fetches),
+                (alpha, perturb, beyond[c], k_beyond, kappa, land),
+                [(half, len(group), rows, lon) for group, order in plans[c] for k in parts_of],
+                scratch,
+                left=2 * fetches,
+            )
+            for k, part in enumerate(parts_of):
+                sums[1 - part].extend(made[k :: len(parts_of)])
         for g, (group, order) in enumerate(plans[c]):
+            name = f"c{c}g{g}"
             offset, weights = apart[c, g]
-            keep, got = scatter(sums[2 * g], sums[2 * g + 1], order)
+            keep, got = scatter(sums[0][g], sums[1][g], order)
             both = keep + got
             both = jnp.stack([both[0] - offset, both[1]])
             got = exchange(both, bits[-1])
@@ -312,25 +394,28 @@
             (perturb, land, *parts[c]),
             [(members, count, rows, lon)] + [(members * count, 4, lon)] * 2,
         )
-        args = [alpha, back, halves(to_partner, to_next), k_beyond, kappa]
-        specs = [VMEM] * len(args)
-        if gradient is not None:
-            args.append(gradient)
-            specs.append(pl.BlockSpec(memory_space=pl.ANY))
-        gradient = pl.pallas_call(
-            functools.partial(adjoint_kernel, c, width),
-            out_shape=jax.ShapeDtypeStruct(alpha.shape, F32),
-            in_specs=specs,
-            out_specs=pl.BlockSpec(memory_space=pl.ANY),
-            scratch_shapes=[
-                pltpu.VMEM((10, rows, lon), F32),
-                pltpu.VMEM((members, lon // LANES, 2 * rows, LANES), F32),
-                pltpu.VMEM((members, count, rows, lon), F32),
-                pltpu.SemaphoreType.DMA((members, count)),
-            ],
-            input_output_aliases={5: 0} if c else {},
-            compiler_params=GRANT,
-        )(*args)
+        spans = ((0, count),)
+        around = halves(to_partner, to_next)
+        for span in spans:
+            args = [alpha, back, around, k_beyond, kappa]
+            specs = [VMEM] * len(args)
+            if gradient is not None:
+                args.append(gradient)
+                specs.append(HERE)
+            gradient = pl.pallas_call(
+                functools.partial(adjoint_kernel, c, width, span),
+                out_shape=jax.ShapeDtypeStruct(alpha.shape, F32),
+                in_specs=specs,
+                out_specs=HERE,
+                scratch_shapes=[
+                    pltpu.VMEM((10, rows, lon), F32),
+                    pltpu.VMEM((members, lon // LANES, 2 * rows, LANES), F32),
+                    pltpu.VMEM((members, span[1] - span[0], rows, lon), F32),
+                    pltpu.SemaphoreType.DMA((members, span[1] - span[0])),
+                ],
+                input_output_aliases={5: 0} if len(args) > 5 else {},
+                compiler_params=GRANT,
+            )(*args)
     misfit = jnp.stack([jnp.concatenate(m, axis=0) for m in misfits], axis=1)
     return gradient, misfit
 

time: 129 us -> 131 us (1.016)
  starting transfers between devices: 33 us -> 39.6 us
  waiting for transfers between devices: 61.8 us -> 57.5 us
  local copies, waits for them, and re-layouts: 7.09 us -> 4.67 us
  Pallas kernels: 22.8 us -> 25.1 us
    ppermute x21, waiting for transfers between devices: 56.1 us -> 49.3 us  [exchange(): return lax.ppermute(x, 'member', [(i, i ^ bit) for i in range(count)])]
    ppermute x4, waiting for transfers between devices: 5.65 us -> 8.18 us  [to_next_chip(): lax.ppermute(x, 'space', [(i, i + 1 if i % 2 else i - 1) for i in range(1...]
    unnamed x20 -> x18, local copies, waits for them, and re-layouts: 6.97 us -> 4.55 us
    ppermute x21, starting transfers between devices: 18.5 us -> 20.9 us  [exchange(): return lax.ppermute(x, 'member', [(i, i ^ bit) for i in range(count)])]
    ppermute x4, starting transfers between devices: 9.37 us -> 11.6 us  [to_next_chip(): lax.ppermute(x, 'space', [(i, i + 1 if i % 2 else i - 1) for i in range(1...]
    pallas_call x5 -> x6, Pallas kernels: 11.3 us -> 13.6 us  [call(): pl.pallas_call(kernel, out_shape=[jax.ShapeDtypeStruct(shape, F32) for sh...]
    ppermute x4, starting transfers between devices: 5.15 us -> 7.07 us  [to_partner_chip(): return lax.ppermute(x, 'space', [(i, i ^ 1) for i in range(ends)])]
  transfers between devices with their start and end apart: 29 -> 29, of which waited for: 18 -> 13; matrix products, arithmetic and copies ran while one was open for 2% -> 2% of each run, Pallas kernels for 9% -> 6%
where the time goes in v2:
time: 131 us
  waiting for transfers between devices  57.5 us (44%)
  starting transfers between devices  39.6 us (30%)
  Pallas kernels  25.1 us (19%)
  local copies, waits for them, and re-layouts  4.67 us (4%)
  other arithmetic  2.65 us (2%)
    ppermute x21, waiting for transfers between devices, exchange(): return lax.ppermute(x, 'member', [(i, i ^ bit) for i in range(count)])  49.3 us
    ppermute x21, starting transfers between devices, exchange(): return lax.ppermute(x, 'member', [(i, i ^ bit) for i in range(count)])  20.9 us
    pallas_call x6, Pallas kernels, call(): pl.pallas_call(kernel, out_shape=[jax.ShapeDtypeStruct(shape, F32) for sh...  13.6 us
    ppermute x4, starting transfers between devices, to_next_chip(): lax.ppermute(x, 'space', [(i, i + 1 if i % 2 else i - 1) for i in range(1...  11.6 us
    pallas_call x2, Pallas kernels, inner(): pl.pallas_call(functools.partial(adjoint_kernel, c, width, span), out_sha...  11.5 us
    ppermute x4, waiting for transfers between devices, to_next_chip(): lax.ppermute(x, 'space', [(i, i + 1 if i % 2 else i - 1) for i in range(1...  8.18 us
    ppermute x4, starting transfers between devices, to_partner_chip(): return lax.ppermute(x, 'space', [(i, i ^ 1) for i in range(ends)])  7.07 us
    unnamed x18, local copies, waits for them, and re-layouts  4.55 us
  transfers between devices with their start and end apart: 29, of which 13 were waited for; matrix products, arithmetic and copies ran while one was open for 2% of the time, Pallas kernels for 6%

profile of v2, /device:TPU:1, one launch (start us, length us, event | category | flops | bytes accessed | tf_op | source)
XLA Modules:
  0.0 130.6 jit_solution(1647239547219573001)
XLA Ops:
  1.7 3.2 %collective-permute-start = (f32[4,2,8,1280]{3,2,0,1:T(8,128)S(1)}, f32[4,2,8,1280]{3,2,0,1:T(8,128)S(1)}, u32[]{:S(2)}, u32[]{:S(2)}) collective-permute-start(f32[4,2,8,1280]{3,2,0,1:T(8,128)S(1)} %copy.10), channel_id=1, source_target_pairs={{0,16},{4,20},{8,24},{12,28},{16,0},{20,4},{24,8},{28,12},{1,17},{... | collective-permute-start | bytes 983048 | tf_op jit(solution)/shard_map/ppermute | solution.py:280
  4.9 1.4 %shard_map.77 = (f32[17,4,1280]{2,1,0:T(4,128)S(1)}, f32[17,4,1280]{2,1,0:T(4,128)S(1)}, f32[16,4,1280]{2,1,0:T(4,128)S(1)}, f32[16,4,1280]{2,1,0:T(4,128)S(1)}) custom-call(f32[2,16,8,1280]{3,2,1,0:T(8,128)} %alpha.11, f32[8,1280]{1,0:T(8,128)} %kappa.11), custom_call_target="tpu_custom_call" | custom-call | tf_op jit(solution)/shard_map/pallas_call | solution.py:268
  7.3 3.0 %collective-permute-start.2 = (f32[16,4,1280]{2,1,0:T(4,128)S(1)}, f32[16,4,1280]{2,1,0:T(4,128)}, u32[]{:S(2)}, u32[]{:S(2)}) collective-permute-start(f32[16,4,1280]{2,1,0:T(4,128)S(1)} %get-tuple-element.30), channel_id=1, source_target_pairs={{1,2},{2,1},{5,6},{6,5},{9,10},{10,9},{13,14},{14,13},{17,18},{18,... | collective-permute-start | bytes 983048 | tf_op jit(solution)/shard_map/ppermute | solution.py:290
  10.5 2.5 %collective-permute-start.4 = (f32[17,4,1280]{2,1,0:T(4,128)S(1)}, f32[17,4,1280]{2,1,0:T(4,128)S(1)}, u32[]{:S(2)}, u32[]{:S(2)}) collective-permute-start(f32[17,4,1280]{2,1,0:T(4,128)S(1)} %get-tuple-element.32), channel_id=1, source_target_pairs={{1,2},{2,1},{5,6},{6,5},{9,10},{10,9},{13,14},{14,13},{17,18},{18,... | collective-permute-start | bytes 1044488 | tf_op jit(solution)/shard_map/ppermute | solution.py:290
  13.1 2.9 %collective-permute-done.2 = f32[16,4,1280]{2,1,0:T(4,128)} collective-permute-done((f32[16,4,1280]{2,1,0:T(4,128)S(1)}, f32[16,4,1280]{2,1,0:T(4,128)}, u32[]{:S(2)}, u32[]{:S(2)}) %collective-permute-start.2) | collective-permute-done | bytes 327712 | tf_op jit(solution)/shard_map/ppermute | solution.py:290
  17.1 2.2 %collective-permute-done = f32[4,2,8,1280]{3,2,0,1:T(8,128)S(1)} collective-permute-done((f32[4,2,8,1280]{3,2,0,1:T(8,128)S(1)}, f32[4,2,8,1280]{3,2,0,1:T(8,128)S(1)}, u32[]{:S(2)}, u32[]{:S(2)}) %collective-permute-start) | collective-permute-done | bytes 327712 | tf_op jit(solution)/shard_map/ppermute | solution.py:280
  21.5 5.2 %shard_map.78 = (f32[4,2,8,1280]{3,2,1,0:T(8,128)S(1)}, f32[4,2,8,1280]{3,2,1,0:T(8,128)S(1)}, f32[4,2,8,1280]{3,2,1,0:T(8,128)S(1)}, f32[4,2,8,1280]{3,2,1,0:T(8,128)S(1)}) custom-call(f32[2,16,8,1280]{3,2,1,0:T(8,128)S(1)} %copy-done.2, bf16[4,2,16,8,1280]{4,3,2,1,0:T(8,128)(2,1)S(1)} %copy-done, f32[16,8,1280]{2,1,0:T(8,128)S(1)} %pad_maximum_fusion.1.beyond, ...), custom_call_target="tpu_custom_call" | custom-call | tf_op jit(solution)/shard_map/pallas_call | solution.py:268
  28.0 2.6 %shard_map.80 = (f32[4,2,8,1280]{3,2,1,0:T(8,128)S(1)}, f32[4,2,8,1280]{3,2,1,0:T(8,128)S(1)}) custom-call(f32[2,16,8,1280]{3,2,1,0:T(8,128)S(1)} %copy-done.2, bf16[4,2,16,8,1280]{4,3,2,1,0:T(8,128)(2,1)S(1)} %copy-done, f32[17,8,1280]{2,1,0:T(8,128)S(1)} %pad_maximum_fusion.beyond, f32[8,1280]{1,0:T(8,128)S(1)} %fusion.13.k_beyond, ...), custom_call_target="tpu_custom_call" | custom-call | tf_op jit(solution)/shard_map/pallas_call | solution.py:268
  30.6 3.5 %shard_map.81 = (f32[4,2,8,1280]{3,2,1,0:T(8,128)S(1)}, f32[4,2,8,1280]{3,2,1,0:T(8,128)S(1)}) custom-call(f32[2,16,8,1280]{3,2,1,0:T(8,128)} %alpha.11, bf16[4,2,16,8,1280]{4,3,2,1,0:T(8,128)(2,1)} %perturb.9, f32[17,8,1280]{2,1,0:T(8,128)S(1)} %pad_maximum_fusion.beyond, f32[8,1280]{1,0:T(8,128)S(1)} %fusion.13.k_beyond, f32[8,1280]{1,0:T(8,128)S(1)} %copy-done.4, ...), custom_call_target="tpu_custom_call" | custom-call | tf_op jit(solution)/shard_map/pallas_call | solution.py:268
  34.1 1.5 %collective-permute-start.10 = (f32[4,2,8,1280]{3,2,1,0:T(8,128)S(1)}, f32[4,2,8,1280]{3,2,1,0:T(8,128)S(1)}, u32[]{:S(2)}, u32[]{:S(2)}) collective-permute-start(f32[4,2,8,1280]{3,2,1,0:T(8,128)S(1)} %get-tuple-element.38), channel_id=1, source_target_pairs={{0,8},{4,12},{8,0},{12,4},{16,24},{20,28},{24,16},{28,20},{1,9},{5... | collective-permute-start | bytes 983048 | tf_op jit(solution)/shard_map/ppermute | solution.py:280
  35.9 1.2 collective-permute-start.22
  37.3 4.7 %collective-permute-done.10 = f32[4,2,8,1280]{3,2,1,0:T(8,128)S(1)} collective-permute-done((f32[4,2,8,1280]{3,2,1,0:T(8,128)S(1)}, f32[4,2,8,1280]{3,2,1,0:T(8,128)S(1)}, u32[]{:S(2)}, u32[]{:S(2)}) %collective-permute-start.10) | collective-permute-done | bytes 327712 | tf_op jit(solution)/shard_map/ppermute | solution.py:280
  42.5 1.3 %collective-permute-done.17 = f32[4,2,8,1280]{3,2,1,0:T(8,128)S(1)} collective-permute-done((f32[4,2,8,1280]{3,2,1,0:T(8,128)S(1)}, f32[4,2,8,1280]{3,2,1,0:T(8,128)S(1)}, u32[]{:S(2)}, u32[]{:S(2)}) %collective-permute-start.17) | collective-permute-done | bytes 327712 | tf_op jit(solution)/shard_map/ppermute | solution.py:280
  44.5 6.3 %collective-permute-done.22 = f32[4,2,8,1280]{3,2,1,0:T(8,128)S(1)} collective-permute-done((f32[4,2,8,1280]{3,2,1,0:T(8,128)S(1)}, f32[4,2,8,1280]{3,2,1,0:T(8,128)S(1)}, u32[]{:S(2)}, u32[]{:S(2)}) %collective-permute-start.22) | collective-permute-done | bytes 327712 | tf_op jit(solution)/shard_map/ppermute | solution.py:280
  51.1 3.5 %collective-permute-start.7 = (f32[2,2,8,1280]{3,2,1,0:T(8,128)S(1)}, f32[2,2,8,1280]{3,2,1,0:T(8,128)S(1)}, u32[]{:S(2)}, u32[]{:S(2)}) collective-permute-start(f32[2,2,8,1280]{3,2,1,0:T(8,128)S(1)} %pad_maximum_fusion.13), channel_id=1, source_target_pairs={{0,16},{4,20},{8,24},{12,28},{16,0},{20,4},{24,8},{28,12},{1,17},{... | collective-permute-start | bytes 491528 | tf_op jit(solution)/shard_map/ppermute | solution.py:280
  54.7 3.0 %collective-permute-start.12 = (f32[2,2,8,1280]{3,2,1,0:T(8,128)S(1)}, f32[2,2,8,1280]{3,2,1,0:T(8,128)S(1)}, u32[]{:S(2)}, u32[]{:S(2)}) collective-permute-start(f32[2,2,8,1280]{3,2,1,0:T(8,128)S(1)} %pad_maximum_fusion.14), channel_id=1, source_target_pairs={{0,16},{4,20},{8,24},{12,28},{16,0},{20,4},{24,8},{28,12},{1,17},{... | collective-permute-start | bytes 491528 | tf_op jit(solution)/shard_map/ppermute | solution.py:280
  57.9 2.4 %collective-permute-start.24 = (f32[2,2,8,1280]{3,2,1,0:T(8,128)S(1)}, f32[2,2,8,1280]{3,2,1,0:T(8,128)S(1)}, u32[]{:S(2)}, u32[]{:S(2)}) collective-permute-start(f32[2,2,8,1280]{3,2,1,0:T(8,128)S(1)} %pad_maximum_fusion.16), channel_id=1, source_target_pairs={{0,16},{4,20},{8,24},{12,28},{16,0},{20,4},{24,8},{28,12},{1,17},{... | collective-permute-start | bytes 491528 | tf_op jit(solution)/shard_map/ppermute | solution.py:280
  60.8 12.8 %collective-permute-done.12 = f32[2,2,8,1280]{3,2,1,0:T(8,128)S(1)} collective-permute-done((f32[2,2,8,1280]{3,2,1,0:T(8,128)S(1)}, f32[2,2,8,1280]{3,2,1,0:T(8,128)S(1)}, u32[]{:S(2)}, u32[]{:S(2)}) %collective-permute-start.12) | collective-permute-done | bytes 163872 | tf_op jit(solution)/shard_map/ppermute | solution.py:280
  73.9 5.3 %collective-permute-done.19 = f32[2,2,8,1280]{3,2,1,0:T(8,128)S(1)} collective-permute-done((f32[2,2,8,1280]{3,2,1,0:T(8,128)S(1)}, f32[2,2,8,1280]{3,2,1,0:T(8,128)S(1)}, u32[]{:S(2)}, u32[]{:S(2)}) %collective-permute-start.19) | collective-permute-done | bytes 163872 | tf_op jit(solution)/shard_map/ppermute | solution.py:280
  79.4 3.4 %collective-permute-done.24 = f32[2,2,8,1280]{3,2,1,0:T(8,128)S(1)} collective-permute-done((f32[2,2,8,1280]{3,2,1,0:T(8,128)S(1)}, f32[2,2,8,1280]{3,2,1,0:T(8,128)S(1)}, u32[]{:S(2)}, u32[]{:S(2)}) %collective-permute-start.24) | collective-permute-done | bytes 163872 | tf_op jit(solution)/shard_map/ppermute | solution.py:280
  83.3 1.5 %collective-permute-start.14 = (f32[4,2,8,1280]{3,2,1,0:T(8,128)S(1)}, f32[4,2,8,1280]{3,2,1,0:T(8,128)S(1)}, u32[]{:S(2)}, u32[]{:S(2)}) collective-permute-start(f32[4,2,8,1280]{3,2,1,0:T(8,128)S(1)} %pad_maximum_fusion.5.refs_2_), channel_id=1, source_target_pairs={{0,8},{4,12},{8,0},{12,4},{16,24},{20,28},{24,16},{28,20},{1,9},{5... | collective-permute-start | bytes 983048 | tf_op jit(solution)/shard_map/ppermute | solution.py:280
  84.9 3.3 %collective-permute-done.20 = f32[2,2,8,1280]{3,2,1,0:T(8,128)S(1)} collective-permute-done((f32[2,2,8,1280]{3,2,1,0:T(8,128)S(1)}, f32[2,2,8,1280]{3,2,1,0:T(8,128)S(1)}, u32[]{:S(2)}, u32[]{:S(2)}) %collective-permute-start.20) | collective-permute-done | bytes 163872 | tf_op jit(solution)/shard_map/ppermute | solution.py:280
  88.5 3.2 %collective-permute-done.25 = f32[2,2,8,1280]{3,2,1,0:T(8,128)S(1)} collective-permute-done((f32[2,2,8,1280]{3,2,1,0:T(8,128)S(1)}, f32[2,2,8,1280]{3,2,1,0:T(8,128)S(1)}, u32[]{:S(2)}, u32[]{:S(2)}) %collective-permute-start.25) | collective-permute-done | bytes 163872 | tf_op jit(solution)/shard_map/ppermute | solution.py:280
  92.0 6.7 %collective-permute-done.14.refs_3_ = f32[4,2,8,1280]{3,2,1,0:T(8,128)S(1)} collective-permute-done((f32[4,2,8,1280]{3,2,1,0:T(8,128)S(1)}, f32[4,2,8,1280]{3,2,1,0:T(8,128)S(1)}, u32[]{:S(2)}, u32[]{:S(2)}) %collective-permute-start.14) | collective-permute-done | bytes 327712 | tf_op jit(solution)/shard_map/ppermute | solution.py:280
  99.1 2.1 %collective-permute-start.15 = (f32[16,4,1280]{2,1,0:T(4,128)S(1)}, f32[16,4,1280]{2,1,0:T(4,128)S(1)}, u32[]{:S(2)}, u32[]{:S(2)}) collective-permute-start(f32[16,4,1280]{2,1,0:T(4,128)S(1)} %get-tuple-element.41), channel_id=1, source_target_pairs={{0,1},{1,0},{2,3},{3,2},{4,5},{5,4},{6,7},{7,6},{8,9},{9,8},{10,11... | collective-permute-start | bytes 983048 | tf_op jit(solution)/shard_map/ppermute | solution.py:285
  101.3 3.0 %collective-permute-start.16 = (f32[16,4,1280]{2,1,0:T(4,128)S(1)}, f32[16,4,1280]{2,1,0:T(4,128)S(1)}, u32[]{:S(2)}, u32[]{:S(2)}) collective-permute-start(f32[16,4,1280]{2,1,0:T(4,128)S(1)} %get-tuple-element.42), channel_id=1, source_target_pairs={{1,2},{2,1},{5,6},{6,5},{9,10},{10,9},{13,14},{14,13},{17,18},{18,... | collective-permute-start | bytes 983048 | tf_op jit(solution)/shard_map/ppermute | solution.py:290
  105.5 3.9 %collective-permute-start.27 = (f32[16,4,1280]{2,1,0:T(4,128)S(1)}, f32[16,4,1280]{2,1,0:T(4,128)S(1)}, u32[]{:S(2)}, u32[]{:S(2)}) collective-permute-start(f32[16,4,1280]{2,1,0:T(4,128)S(1)} %get-tuple-element.52), channel_id=1, source_target_pairs={{0,1},{1,0},{2,3},{3,2},{4,5},{5,4},{6,7},{7,6},{8,9},{9,8},{10,11... | collective-permute-start | bytes 983048 | tf_op jit(solution)/shard_map/ppermute | solution.py:285
  109.4 3.0 %collective-permute-start.28 = (f32[16,4,1280]{2,1,0:T(4,128)S(1)}, f32[16,4,1280]{2,1,0:T(4,128)S(1)}, u32[]{:S(2)}, u32[]{:S(2)}) collective-permute-start(f32[16,4,1280]{2,1,0:T(4,128)S(1)} %get-tuple-element.53), channel_id=1, source_target_pairs={{1,2},{2,1},{5,6},{6,5},{9,10},{10,9},{13,14},{14,13},{17,18},{18,... | collective-permute-start | bytes 983048 | tf_op jit(solution)/shard_map/ppermute | solution.py:290
  112.7 5.1 %collective-permute-done.28 = f32[16,4,1280]{2,1,0:T(4,128)S(1)} collective-permute-done((f32[16,4,1280]{2,1,0:T(4,128)S(1)}, f32[16,4,1280]{2,1,0:T(4,128)S(1)}, u32[]{:S(2)}, u32[]{:S(2)}) %collective-permute-start.28) | collective-permute-done | bytes 327712 | tf_op jit(solution)/shard_map/ppermute | solution.py:290
  118.0 1.1 copy-done.3
  119.1 5.8 %shard_map.83.refs_0_ = f32[2,16,8,1280]{3,2,1,0:T(8,128)} custom-call(f32[2,16,8,1280]{3,2,1,0:T(8,128)S(1)} %copy-done.3, f32[2,8,8,1280]{3,2,1,0:T(8,128)S(1)} %get-tuple-element.51.back, f32[16,8,1280]{2,1,0:T(8,128)S(1)} %pad_maximum_fusion.3.beyond, f32[8,1280]{1,0:T(8,128)S(1)} %fusion.13.k_beyond, f32[8,1280]{1,0:T(8,128)S(1)} %copy-done.4), custom_call_target="tpu_custom_call" | custom-call | tf_op jit(solution)/shard_map/pallas_call | solution.py:405
  124.9 5.8 %shard_map.84 = f32[2,16,8,1280]{3,2,1,0:T(8,128)} custom-call(f32[2,16,8,1280]{3,2,1,0:T(8,128)S(1)} %copy-done.3, f32[2,8,8,1280]{3,2,1,0:T(8,128)S(1)} %get-tuple-element.40.back, f32[16,8,1280]{2,1,0:T(8,128)S(1)} %pad_maximum_fusion.2.beyond, f32[8,1280]{1,0:T(8,128)S(1)} %fusion.13.k_beyond, ...), custom_call_target="tpu_custom_call", output_to_operand_aliasing={{}: (5, {})} | custom-call | tf_op jit(solution)/shard_map/pallas_call | solution.py:405
  (101 shorter events, 12.9 us)
Async XLA Ops:
  0.6 12.4 %copy-start.6 = (f32[4,2,8,1280]{3,2,1,0:T(8,128)S(1)}, f32[4,2,8,1280]{3,2,1,0:T(8,128)}, u32[]{:S(2)}) copy-start(f32[4,2,8,1280]{3,2,1,0:T(8,128)} %param.10) | copy-start | bytes 983044
  0.6 12.4 %copy-start.7 = (f32[4,2,8,1280]{3,2,1,0:T(8,128)S(1)}, f32[4,2,8,1280]{3,2,1,0:T(8,128)}, u32[]{:S(2)}) copy-start(f32[4,2,8,1280]{3,2,1,0:T(8,128)} %param.11) | copy-start | bytes 983044
  1.7 17.6 %collective-permute-start = (f32[4,2,8,1280]{3,2,0,1:T(8,128)S(1)}, f32[4,2,8,1280]{3,2,0,1:T(8,128)S(1)}, u32[]{:S(2)}, u32[]{:S(2)}) collective-permute-start(f32[4,2,8,1280]{3,2,0,1:T(8,128)S(1)} %copy.10), channel_id=1, source_target_pairs={{0,16},{4,20},{8,24},{12,28},{16,0},{20,4},{24,8},{28,12},{1,17},{... | collective-permute-start | bytes 983048 | tf_op jit(solution)/shard_map/ppermute | solution.py:280
  6.3 6.8 %collective-permute-start.1 = (f32[16,4,1280]{2,1,0:T(4,128)S(1)}, f32[16,4,1280]{2,1,0:T(4,128)}, u32[]{:S(2)}, u32[]{:S(2)}) collective-permute-start(f32[16,4,1280]{2,1,0:T(4,128)S(1)} %get-tuple-element.29), channel_id=1, source_target_pairs={{0,1},{1,0},{2,3},{3,2},{4,5},{5,4},{6,7},{7,6},{8,9},{9,8},{10,11... | collective-permute-start | bytes 983048 | tf_op jit(solution)/shard_map/ppermute | solution.py:285
  7.3 8.7 %collective-permute-start.2 = (f32[16,4,1280]{2,1,0:T(4,128)S(1)}, f32[16,4,1280]{2,1,0:T(4,128)}, u32[]{:S(2)}, u32[]{:S(2)}) collective-permute-start(f32[16,4,1280]{2,1,0:T(4,128)S(1)} %get-tuple-element.30), channel_id=1, source_target_pairs={{1,2},{2,1},{5,6},{6,5},{9,10},{10,9},{13,14},{14,13},{17,18},{18,... | collective-permute-start | bytes 983048 | tf_op jit(solution)/shard_map/ppermute | solution.py:290
  10.4 9.2 %collective-permute-start.3 = (f32[17,4,1280]{2,1,0:T(4,128)S(1)}, f32[17,4,1280]{2,1,0:T(4,128)S(1)}, u32[]{:S(2)}, u32[]{:S(2)}) collective-permute-start(f32[17,4,1280]{2,1,0:T(4,128)S(1)} %get-tuple-element.31), channel_id=1, source_target_pairs={{0,1},{1,0},{2,3},{3,2},{4,5},{5,4},{6,7},{7,6},{8,9},{9,8},{10,11... | collective-permute-start | bytes 1044488 | tf_op jit(solution)/shard_map/ppermute | solution.py:285
  10.5 9.3 %collective-permute-start.4 = (f32[17,4,1280]{2,1,0:T(4,128)S(1)}, f32[17,4,1280]{2,1,0:T(4,128)S(1)}, u32[]{:S(2)}, u32[]{:S(2)}) collective-permute-start(f32[17,4,1280]{2,1,0:T(4,128)S(1)} %get-tuple-element.32), channel_id=1, source_target_pairs={{1,2},{2,1},{5,6},{6,5},{9,10},{10,9},{13,14},{14,13},{17,18},{18,... | collective-permute-start | bytes 1044488 | tf_op jit(solution)/shard_map/ppermute | solution.py:290
  26.7 10.4 %collective-permute-start.5 = (f32[4,2,8,1280]{3,2,1,0:T(8,128)S(1)}, f32[4,2,8,1280]{3,2,1,0:T(8,128)S(1)}, u32[]{:S(2)}, u32[]{:S(2)}) collective-permute-start(f32[4,2,8,1280]{3,2,1,0:T(8,128)S(1)} %get-tuple-element.34), channel_id=1, source_target_pairs={{0,4},{4,0},{8,12},{12,8},{16,20},{20,16},{24,28},{28,24},{1,5},{5... | collective-permute-start | bytes 983048 | tf_op jit(solution)/shard_map/ppermute | solution.py:280
  34.1 7.8 %collective-permute-start.10 = (f32[4,2,8,1280]{3,2,1,0:T(8,128)S(1)}, f32[4,2,8,1280]{3,2,1,0:T(8,128)S(1)}, u32[]{:S(2)}, u32[]{:S(2)}) collective-permute-start(f32[4,2,8,1280]{3,2,1,0:T(8,128)S(1)} %get-tuple-element.38), channel_id=1, source_target_pairs={{0,8},{4,12},{8,0},{12,4},{16,24},{20,28},{24,16},{28,20},{1,9},{5... | collective-permute-start | bytes 983048 | tf_op jit(solution)/shard_map/ppermute | solution.py:280
  35.6 8.2 %collective-permute-start.17 = (f32[4,2,8,1280]{3,2,1,0:T(8,128)S(1)}, f32[4,2,8,1280]{3,2,1,0:T(8,128)S(1)}, u32[]{:S(2)}, u32[]{:S(2)}) collective-permute-start(f32[4,2,8,1280]{3,2,1,0:T(8,128)S(1)} %get-tuple-element.45), channel_id=1, source_target_pairs={{0,4},{4,0},{8,12},{12,8},{16,20},{20,16},{24,28},{28,24},{1,5},{5... | collective-permute-start | bytes 983048 | tf_op jit(solution)/shard_map/ppermute | solution.py:280
  35.9 15.0 %collective-permute-start.22 = (f32[4,2,8,1280]{3,2,1,0:T(8,128)S(1)}, f32[4,2,8,1280]{3,2,1,0:T(8,128)S(1)}, u32[]{:S(2)}, u32[]{:S(2)}) collective-permute-start(f32[4,2,8,1280]{3,2,1,0:T(8,128)S(1)} %get-tuple-element.49), channel_id=1, source_target_pairs={{0,4},{4,0},{8,12},{12,8},{16,20},{20,16},{24,28},{28,24},{1,5},{5... | collective-permute-start | bytes 983048 | tf_op jit(solution)/shard_map/ppermute | solution.py:280
  37.1 13.9 %collective-permute-start.6 = (f32[2,2,8,1280]{3,2,1,0:T(8,128)S(1)}, f32[2,2,8,1280]{3,2,1,0:T(8,128)S(1)}, u32[]{:S(2)}, u32[]{:S(2)}) collective-permute-start(f32[2,2,8,1280]{3,2,1,0:T(8,128)S(1)} %slice_add_fusion.6), channel_id=1, source_target_pairs={{0,8},{4,12},{8,0},{12,4},{16,24},{20,28},{24,16},{28,20},{1,9},{5... | collective-permute-start | bytes 491528 | tf_op jit(solution)/shard_map/ppermute | solution.py:280
  41.9 12.6 %collective-permute-start.11 = (f32[2,2,8,1280]{3,2,1,0:T(8,128)S(1)}, f32[2,2,8,1280]{3,2,1,0:T(8,128)S(1)}, u32[]{:S(2)}, u32[]{:S(2)}) collective-permute-start(f32[2,2,8,1280]{3,2,1,0:T(8,128)S(1)} %slice_add_fusion.4), channel_id=1, source_target_pairs={{0,4},{4,0},{8,12},{12,8},{16,20},{20,16},{24,28},{28,24},{1,5},{5... | collective-permute-start | bytes 491528 | tf_op jit(solution)/shard_map/ppermute | solution.py:280
  43.9 13.8 %collective-permute-start.18 = (f32[2,2,8,1280]{3,2,1,0:T(8,128)S(1)}, f32[2,2,8,1280]{3,2,1,0:T(8,128)S(1)}, u32[]{:S(2)}, u32[]{:S(2)}) collective-permute-start(f32[2,2,8,1280]{3,2,1,0:T(8,128)S(1)} %slice_add_fusion.2), channel_id=1, source_target_pairs={{0,8},{4,12},{8,0},{12,4},{16,24},{20,28},{24,16},{28,20},{1,9},{5... | collective-permute-start | bytes 491528 | tf_op jit(solution)/shard_map/ppermute | solution.py:280
  50.9 6.9 %collective-permute-start.23 = (f32[2,2,8,1280]{3,2,1,0:T(8,128)S(1)}, f32[2,2,8,1280]{3,2,1,0:T(8,128)S(1)}, u32[]{:S(2)}, u32[]{:S(2)}) collective-permute-start(f32[2,2,8,1280]{3,2,1,0:T(8,128)S(1)} %slice_add_fusion), channel_id=1, source_target_pairs={{0,8},{4,12},{8,0},{12,4},{16,24},{20,28},{24,16},{28,20},{1,9},{5... | collective-permute-start | bytes 491528 | tf_op jit(solution)/shard_map/ppermute | solution.py:280
  51.1 9.2 %collective-permute-start.7 = (f32[2,2,8,1280]{3,2,1,0:T(8,128)S(1)}, f32[2,2,8,1280]{3,2,1,0:T(8,128)S(1)}, u32[]{:S(2)}, u32[]{:S(2)}) collective-permute-start(f32[2,2,8,1280]{3,2,1,0:T(8,128)S(1)} %pad_maximum_fusion.13), channel_id=1, source_target_pairs={{0,16},{4,20},{8,24},{12,28},{16,0},{20,4},{24,8},{28,12},{1,17},{... | collective-permute-start | bytes 491528 | tf_op jit(solution)/shard_map/ppermute | solution.py:280
  54.7 18.9 %collective-permute-start.12 = (f32[2,2,8,1280]{3,2,1,0:T(8,128)S(1)}, f32[2,2,8,1280]{3,2,1,0:T(8,128)S(1)}, u32[]{:S(2)}, u32[]{:S(2)}) collective-permute-start(f32[2,2,8,1280]{3,2,1,0:T(8,128)S(1)} %pad_maximum_fusion.14), channel_id=1, source_target_pairs={{0,16},{4,20},{8,24},{12,28},{16,0},{20,4},{24,8},{28,12},{1,17},{... | collective-permute-start | bytes 491528 | tf_op jit(solution)/shard_map/ppermute | solution.py:280
  57.7 21.6 %collective-permute-start.19 = (f32[2,2,8,1280]{3,2,1,0:T(8,128)S(1)}, f32[2,2,8,1280]{3,2,1,0:T(8,128)S(1)}, u32[]{:S(2)}, u32[]{:S(2)}) collective-permute-start(f32[2,2,8,1280]{3,2,1,0:T(8,128)S(1)} %pad_maximum_fusion.15), channel_id=1, source_target_pairs={{0,16},{4,20},{8,24},{12,28},{16,0},{20,4},{24,8},{28,12},{1,17},{... | collective-permute-start | bytes 491528 | tf_op jit(solution)/shard_map/ppermute | solution.py:280
  57.9 24.9 %collective-permute-start.24 = (f32[2,2,8,1280]{3,2,1,0:T(8,128)S(1)}, f32[2,2,8,1280]{3,2,1,0:T(8,128)S(1)}, u32[]{:S(2)}, u32[]{:S(2)}) collective-permute-start(f32[2,2,8,1280]{3,2,1,0:T(8,128)S(1)} %pad_maximum_fusion.16), channel_id=1, source_target_pairs={{0,16},{4,20},{8,24},{12,28},{16,0},{20,4},{24,8},{28,12},{1,17},{... | collective-permute-start | bytes 491528 | tf_op jit(solution)/shard_map/ppermute | solution.py:280
  60.4 22.6 %collective-permute-start.8 = (f32[2,2,8,1280]{3,2,1,0:T(8,128)S(1)}, f32[2,2,8,1280]{3,2,1,0:T(8,128)S(1)}, u32[]{:S(2)}, u32[]{:S(2)}) collective-permute-start(f32[2,2,8,1280]{3,2,1,0:T(8,128)S(1)} %add_multiply_fusion.3), channel_id=1, source_target_pairs={{0,8},{4,12},{8,0},{12,4},{16,24},{20,28},{24,16},{28,20},{1,9},{5... | collective-permute-start | bytes 491528 | tf_op jit(solution)/shard_map/ppermute | solution.py:280
  73.7 9.7 %collective-permute-start.13 = (f32[2,2,8,1280]{3,2,1,0:T(8,128)S(1)}, f32[2,2,8,1280]{3,2,1,0:T(8,128)S(1)}, u32[]{:S(2)}, u32[]{:S(2)}) collective-permute-start(f32[2,2,8,1280]{3,2,1,0:T(8,128)S(1)} %add_multiply_fusion.2), channel_id=1, source_target_pairs={{0,4},{4,0},{8,12},{12,8},{16,20},{20,16},{24,28},{28,24},{1,5},{5... | collective-permute-start | bytes 491528 | tf_op jit(solution)/shard_map/ppermute | solution.py:280
  79.3 8.8 %collective-permute-start.20 = (f32[2,2,8,1280]{3,2,1,0:T(8,128)S(1)}, f32[2,2,8,1280]{3,2,1,0:T(8,128)S(1)}, u32[]{:S(2)}, u32[]{:S(2)}) collective-permute-start(f32[2,2,8,1280]{3,2,1,0:T(8,128)S(1)} %add_multiply_fusion.1), channel_id=1, source_target_pairs={{0,8},{4,12},{8,0},{12,4},{16,24},{20,28},{24,16},{28,20},{1,9},{5... | collective-permute-start | bytes 491528 | tf_op jit(solution)/shard_map/ppermute | solution.py:280
  82.9 8.8 %collective-permute-start.25 = (f32[2,2,8,1280]{3,2,1,0:T(8,128)S(1)}, f32[2,2,8,1280]{3,2,1,0:T(8,128)S(1)}, u32[]{:S(2)}, u32[]{:S(2)}) collective-permute-start(f32[2,2,8,1280]{3,2,1,0:T(8,128)S(1)} %add_multiply_fusion), channel_id=1, source_target_pairs={{0,8},{4,12},{8,0},{12,4},{16,24},{20,28},{24,16},{28,20},{1,9},{5... | collective-permute-start | bytes 491528 | tf_op jit(solution)/shard_map/ppermute | solution.py:280
  83.0 15.7 %copy-start.1 = (bf16[4,2,16,8,1280]{4,3,2,1,0:T(8,128)(2,1)S(1)}, bf16[4,2,16,8,1280]{4,3,2,1,0:T(8,128)(2,1)}, u32[]{:S(2)}) copy-start(bf16[4,2,16,8,1280]{4,3,2,1,0:T(8,128)(2,1)} %perturb.9) | copy-start | bytes 7864324
  83.0 9.0 %collective-permute-start.9 = (f32[4,2,8,1280]{3,2,1,0:T(8,128)S(1)}, f32[4,2,8,1280]{3,2,1,0:T(8,128)S(1)}, u32[]{:S(2)}, u32[]{:S(2)}) collective-permute-start(f32[4,2,8,1280]{3,2,1,0:T(8,128)S(1)} %pad_maximum_fusion.4.refs_0_), channel_id=1, source_target_pairs={{0,4},{4,0},{8,12},{12,8},{16,20},{20,16},{24,28},{28,24},{1,5},{5... | collective-permute-start | bytes 983048 | tf_op jit(solution)/shard_map/ppermute | solution.py:280
  83.3 15.4 %collective-permute-start.14 = (f32[4,2,8,1280]{3,2,1,0:T(8,128)S(1)}, f32[4,2,8,1280]{3,2,1,0:T(8,128)S(1)}, u32[]{:S(2)}, u32[]{:S(2)}) collective-permute-start(f32[4,2,8,1280]{3,2,1,0:T(8,128)S(1)} %pad_maximum_fusion.5.refs_2_), channel_id=1, source_target_pairs={{0,8},{4,12},{8,0},{12,4},{16,24},{20,28},{24,16},{28,20},{1,9},{5... | collective-permute-start | bytes 983048 | tf_op jit(solution)/shard_map/ppermute | solution.py:280
  88.2 16.9 %collective-permute-start.21 = (f32[4,2,8,1280]{3,2,1,0:T(8,128)S(1)}, f32[4,2,8,1280]{3,2,1,0:T(8,128)S(1)}, u32[]{:S(2)}, u32[]{:S(2)}) collective-permute-start(f32[4,2,8,1280]{3,2,1,0:T(8,128)S(1)} %pad_maximum_fusion.6.refs_0_), channel_id=1, source_target_pairs={{0,4},{4,0},{8,12},{12,8},{16,20},{20,16},{24,28},{28,24},{1,5},{5... | collective-permute-start | bytes 983048 | tf_op jit(solution)/shard_map/ppermute | solution.py:280
  91.7 13.4 %collective-permute-start.26 = (f32[4,2,8,1280]{3,2,1,0:T(8,128)S(1)}, f32[4,2,8,1280]{3,2,1,0:T(8,128)S(1)}, u32[]{:S(2)}, u32[]{:S(2)}) collective-permute-start(f32[4,2,8,1280]{3,2,1,0:T(8,128)S(1)} %pad_maximum_fusion.7.refs_2_), channel_id=1, source_target_pairs={{0,4},{4,0},{8,12},{12,8},{16,20},{20,16},{24,28},{28,24},{1,5},{5... | collective-permute-start | bytes 983048 | tf_op jit(solution)/shard_map/ppermute | solution.py:280
  99.1 13.3 %collective-permute-start.15 = (f32[16,4,1280]{2,1,0:T(4,128)S(1)}, f32[16,4,1280]{2,1,0:T(4,128)S(1)}, u32[]{:S(2)}, u32[]{:S(2)}) collective-permute-start(f32[16,4,1280]{2,1,0:T(4,128)S(1)} %get-tuple-element.41), channel_id=1, source_target_pairs={{0,1},{1,0},{2,3},{3,2},{4,5},{5,4},{6,7},{7,6},{8,9},{9,8},{10,11... | collective-permute-start | bytes 983048 | tf_op jit(solution)/shard_map/ppermute | solution.py:285
  101.3 11.2 %collective-permute-start.16 = (f32[16,4,1280]{2,1,0:T(4,128)S(1)}, f32[16,4,1280]{2,1,0:T(4,128)S(1)}, u32[]{:S(2)}, u32[]{:S(2)}) collective-permute-start(f32[16,4,1280]{2,1,0:T(4,128)S(1)} %get-tuple-element.42), channel_id=1, source_target_pairs={{1,2},{2,1},{5,6},{6,5},{9,10},{10,9},{13,14},{14,13},{17,18},{18,... | collective-permute-start | bytes 983048 | tf_op jit(solution)/shard_map/ppermute | solution.py:290
  105.5 7.1 %collective-permute-start.27 = (f32[16,4,1280]{2,1,0:T(4,128)S(1)}, f32[16,4,1280]{2,1,0:T(4,128)S(1)}, u32[]{:S(2)}, u32[]{:S(2)}) collective-permute-start(f32[16,4,1280]{2,1,0:T(4,128)S(1)} %get-tuple-element.52), channel_id=1, source_target_pairs={{0,1},{1,0},{2,3},{3,2},{4,5},{5,4},{6,7},{7,6},{8,9},{9,8},{10,11... | collective-permute-start | bytes 983048 | tf_op jit(solution)/shard_map/ppermute | solution.py:285
  109.4 8.4 %collective-permute-start.28 = (f32[16,4,1280]{2,1,0:T(4,128)S(1)}, f32[16,4,1280]{2,1,0:T(4,128)S(1)}, u32[]{:S(2)}, u32[]{:S(2)}) collective-permute-start(f32[16,4,1280]{2,1,0:T(4,128)S(1)} %get-tuple-element.53), channel_id=1, source_target_pairs={{1,2},{2,1},{5,6},{6,5},{9,10},{10,9},{13,14},{14,13},{17,18},{18,... | collective-permute-start | bytes 983048 | tf_op jit(solution)/shard_map/ppermute | solution.py:290
  (5 other events, 8.7 us)
